TPU v7x, 256 devices: a whole 4x4x8 slice. The times are simulated.
256 devices in a mesh: group: 8 (over x, y_lo), dev: 32 (over y_hi, z, core).
Axes of the slice: x: 4, y: 4 (y_hi: 2, y_lo: 2; y = y_hi * 2 + y_lo), z: 8, core: 2. Of those that a mesh axis runs over, the one named last changes fastest.
Arguments:
- particles: float32 [512, 16, 8, 128], P(('group', 'dev')), as said below
- counts: int32 [512, 16], P(('group', 'dev')), may hold values from 0 to 128, as said below
Outputs:
- density: float32 [512, 16, 128], P(('group', 'dev'))
- density_rate: float32 [512, 16, 128], P(('group', 'dev'))
- acceleration: float32 [512, 16, 2, 128], P(('group', 'dev'))
Inputs may be any that keep to these rules, and one draw needn't show every extreme that they name: The first counts slots of a cell hold its live particles. `particles`: every slot's mass (component 4) is positive and every smoothing length (component 5) lies within 0.3 to 0.5.
All inputs are finite; a program needn't handle non-finite values.
Results may differ from a plain program's by a relative error of at most 0.0001.
Values sent between devices are 32-bit elements; how exact they have to be, the bound alone decides.
A program may use at most 64 MiB of HBM per device.

v0:
```python
import math

import jax
import jax.numpy as jnp
from jax import lax
from jax.sharding import PartitionSpec as P

wendland_norm = 7.0 / (4.0 * math.pi)
gradient_norm = 35.0 / (4.0 * math.pi)
sound_factor = 10.0
visc_softening = 0.01
neighbour_steps = ((-1, -1), (-1, 0), (-1, 1), (0, -1), (0, 0), (0, 1), (1, -1), (1, 0), (1, 1))


def extended(array, sides, width):
    for axis, dim in sides:
        peers, length = (lax.axis_size(axis), array.shape[dim])
        up = [(i, (i + 1) % peers) for i in range(peers - 1)]
        down = [(j, i) for i, j in up]
        last = lax.slice_in_dim(array, length - width, length, axis=dim)
        first = lax.slice_in_dim(array, 0, width, axis=dim)
        before = lax.ppermute(last, axis, up)
        after = lax.ppermute(first, axis, down)
        array = jnp.concatenate([before, array, after], axis=dim)
    return array


def pair_geometry(centre, neighbour, step_x, step_y):
    sep_x = centre[:, 0, :, None] - neighbour[:, 0, None, :] - step_x
    sep_y = centre[:, 1, :, None] - neighbour[:, 1, None, :] - step_y
    pair_h = 0.5 * (centre[:, 5, :, None] + neighbour[:, 5, None, :])
    dist_sq = sep_x * sep_x + sep_y * sep_y
    radius_ratio = jnp.sqrt(dist_sq) / pair_h
    falloff = jnp.maximum(1.0 - 0.5 * radius_ratio, 0.0)
    falloff_cube = falloff * falloff * falloff
    h_square = pair_h * pair_h
    kernel = wendland_norm / h_square * falloff_cube * falloff * (2.0 * radius_ratio + 1.0)
    gradient = -gradient_norm / (h_square * h_square) * falloff_cube
    return (sep_x, sep_y, pair_h, dist_sq, kernel, gradient)


def density_terms(centre, neighbour, step_x, step_y):
    sep_x, sep_y, pair_h, dist_sq, kernel, gradient = pair_geometry(
        centre, neighbour, step_x, step_y
    )
    mass_j = neighbour[:, 4, None, :]
    closing = (centre[:, 2, :, None] - neighbour[:, 2, None, :]) * sep_x + (
        centre[:, 3, :, None] - neighbour[:, 3, None, :]
    ) * sep_y
    return (jnp.sum(mass_j * kernel, axis=-1), jnp.sum(mass_j * closing * gradient, axis=-1))


def force_terms(centre, centre_aux, neighbour, neighbour_aux, step_x, step_y, sound):
    sep_x, sep_y, pair_h, dist_sq, kernel, gradient = pair_geometry(
        centre, neighbour, step_x, step_y
    )
    mass_j = neighbour[:, 4, None, :]
    closing = (centre[:, 2, :, None] - neighbour[:, 2, None, :]) * sep_x + (
        centre[:, 3, :, None] - neighbour[:, 3, None, :]
    ) * sep_y
    approach = jnp.minimum(closing, 0.0) / (dist_sq + visc_softening * pair_h * pair_h)
    alpha_pair = 0.5 * (centre[:, 7, :, None] + neighbour[:, 7, None, :])
    rho_pair = 0.5 * (centre_aux[:, 0, :, None] + neighbour_aux[:, 0, None, :])
    viscous = -alpha_pair * sound * pair_h * approach / rho_pair
    coeff = centre_aux[:, 1, :, None] + neighbour_aux[:, 1, None, :] + viscous
    weight = mass_j * coeff * gradient
    accel_x = -jnp.sum(weight * sep_x, axis=-1)
    accel_y = -jnp.sum(weight * sep_y, axis=-1)
    return jnp.stack([accel_x, accel_y], axis=1)


def pressure_fields(density_raw, cells, live_slots, sound):
    rho_safe = jnp.where(live_slots, density_raw, 1.0)
    pressure_term = jnp.where(
        live_slots, sound * sound * (density_raw - cells[:, :, 6, :]) / (rho_safe * rho_safe), 0.0
    )
    return (rho_safe, pressure_term)


def pad_rows(field):
    widths = [(0, 0)] * field.ndim
    widths[1] = (1, 1)
    return jnp.pad(field, widths)


def cut_block(padded, column_at, row_start, block_rows):
    plane = lax.dynamic_index_in_dim(padded, column_at, 0, keepdims=False)
    return lax.dynamic_slice_in_dim(plane, row_start, block_rows, 0)


def block_layout(padded):
    row_total = padded.shape[1] - 2
    block_rows = math.gcd(row_total, 16)
    return (row_total, block_rows, row_total // block_rows)


def column_fields(padded, first_col, col_total):
    row_total, block_rows, per_column = block_layout(padded)
    slot_total = padded.shape[-1]
    empty_sums = (
        jnp.zeros((block_rows, slot_total), jnp.float32),
        jnp.zeros((block_rows, slot_total), jnp.float32),
    )

    def column_locate(block_id):
        return (first_col + block_id // per_column, block_id % per_column * block_rows + 1)

    def column_compute(block_id):
        column_at, row_start = column_locate(block_id)
        centre = cut_block(padded, column_at, row_start, block_rows)
        density_sum, rate_sum = empty_sums
        for step_x, step_y in neighbour_steps:
            neighbour = cut_block(padded, column_at + step_x, row_start + step_y, block_rows)
            density_part, rate_part = density_terms(centre, neighbour, step_x, step_y)
            density_sum = density_sum + density_part
            rate_sum = rate_sum + rate_part
        return (density_sum, rate_sum)

    def column_one_block(block_id):
        return column_compute(block_id)

    density_blocks, rate_blocks = lax.map(
        column_one_block, jnp.arange(col_total * per_column, dtype=jnp.int32)
    )
    return (density_blocks, rate_blocks)


def force_fields(padded, first_col, aux_padded, aux_first, col_total, sound):
    row_total, block_rows, per_column = block_layout(padded)
    slot_total = padded.shape[-1]
    empty_accel = jnp.zeros((block_rows, 2, slot_total), jnp.float32)

    def force_locate(block_id):
        return (block_id // per_column, block_id % per_column * block_rows + 1)

    def force_compute(block_id):
        column_rel, row_start = force_locate(block_id)
        centre = cut_block(padded, first_col + column_rel, row_start, block_rows)
        centre_aux = cut_block(aux_padded, aux_first + column_rel, row_start, block_rows)
        accel_sum = empty_accel
        for step_x, step_y in neighbour_steps:
            neighbour = cut_block(
                padded, first_col + column_rel + step_x, row_start + step_y, block_rows
            )
            neighbour_aux = cut_block(
                aux_padded, aux_first + column_rel + step_x, row_start + step_y, block_rows
            )
            accel_sum = accel_sum + force_terms(
                centre, centre_aux, neighbour, neighbour_aux, step_x, step_y, sound
            )
        return accel_sum

    def force_one_block(block_id):
        return force_compute(block_id)

    accel_blocks = lax.map(force_one_block, jnp.arange(col_total * per_column, dtype=jnp.int32))
    return accel_blocks


def on_device(particles, counts):
    columns = particles.shape[0]
    slot_ids = jnp.arange(particles.shape[3], dtype=jnp.int32)
    live_slots = slot_ids[None, None, :] < counts[:, :, None]
    comp_ids = jnp.arange(particles.shape[2], dtype=jnp.int32)[None, None, :, None]
    masked = jnp.where((comp_ids == 4) & jnp.logical_not(live_slots[:, :, None, :]), 0.0, particles)
    particle_speed = jnp.sqrt(
        particles[:, :, 2, :] * particles[:, :, 2, :]
        + particles[:, :, 3, :] * particles[:, :, 3, :]
    )
    local_top = jnp.max(jnp.where(live_slots, particle_speed, 0.0))
    sound = sound_factor * lax.pmax(local_top, ("group", "dev"))
    ghost_cells = extended(masked, ((("group", "dev"), 0),), 1)
    padded = pad_rows(ghost_cells)
    density_raw, rate_raw = column_fields(padded, 1, columns)
    rho_safe, pressure_term = pressure_fields(density_raw, masked, live_slots, sound)
    auxiliary = jnp.stack([rho_safe, pressure_term], axis=2)
    aux_ghost = extended(auxiliary, ((("group", "dev"), 0),), 1)
    aux_padded = pad_rows(aux_ghost)
    accel_raw = force_fields(padded, 1, aux_padded, 1, columns, sound)
    density = jnp.where(live_slots, density_raw, 0.0)
    density_rate = jnp.where(live_slots, rate_raw, 0.0)
    acceleration = jnp.where(live_slots[:, :, None, :], accel_raw, 0.0)
    return (density, density_rate, acceleration)


def solution(mesh):
    return jax.shard_map(
        on_device,
        mesh=mesh,
        in_specs=(P(("group", "dev"), None, None, None), P(("group", "dev"), None)),
        out_specs=(
            P(("group", "dev"), None, None),
            P(("group", "dev"), None, None),
            P(("group", "dev"), None, None, None),
        ),
        check_vma=False,
    )
```

profile of v0, /device:TPU:1, one launch (start us, length us, event | category | flops | bytes accessed | tf_op | source)
XLA Modules:
  0.0 226.1 jit_solution(9924892327983139151)
XLA Ops:
  2.4 4.9 %collective-permute-start = (f32[1,16,8,128]{3,1,0,2:T(8,128)S(1)}, f32[1,16,8,128]{3,1,0,2:T(8,128)S(1)}, u32[]{:S(2)}, u32[]{:S(2)}) collective-permute-start(f32[1,16,8,128]{3,1,0,2:T(8,128)S(1)} %get-tuple-element.740), channel_id=1, source_target_pairs={{0,1},{1,2},{2,3},{3,4},{4,5},{5,6},{6,7},{7,8},{8,9},{9,10},{10,1... | collective-permute-start | bytes 196616 | tf_op jit(solution)/shard_map/ppermute | solution.py:22
  9.9 79.6 %pmax.7 = f32[]{:T(128)} all-reduce(f32[]{:T(128)} %fusion.236), channel_id=1, replica_groups=mesh['group'=8,'dev'=32] {'group','dev'}, use_global_device_ids=true, to_apply=%region_21.22 | all-reduce | flops 1 | bytes 8 | tf_op jit(solution)/shard_map/pmax | solution.py:171
  90.8 49.2 %while.34 = (s32[]{:T(128)}, f32[2,16,128]{2,1,0:T(8,128)S(1)}, f32[2,16,128]{2,1,0:T(8,128)S(1)}, s32[2]{0:T(128)S(1)}, f32[4,18,8,128]{3,1,2,0:T(8,128)S(1)}) while((s32[]{:T(128)}, f32[2,16,128]{2,1,0:T(8,128)S(1)}, f32[2,16,128]{2,1,0:T(8,128)S(1)}, s32[2]{0:T(128)S(1)}, f32[4,18,8,128]{3,1,2,0:T(8,128)S(1)}) %tuple.405), condition=%wide.region_19.20_spmd.clone, body=%wide.region_0.19_spmd.sunk.clone | while | flops 80998416 | bytes 2941195 | solution.py:122
  96.1 4.3 %multiply_reduce_fusion.39 = (f32[16,128]{1,0:T(8,128)S(1)}, f32[16,128]{1,0:T(8,128)S(1)}, f32[16,128]{1,0:T(8,128)S(1)}, f32[16,128]{1,0:T(8,128)S(1)}) fusion(f32[16,128]{1,0:T(8,128)S(1)} %get-tuple-element.1276, f32[16,128]{1,0:T(8,128)S(1)} %get-tuple-element.1226, f32[16,128]{1,0:T(8,128)S(1)} %get-tuple-element.1277, ...), kind=kLoop, calls=%fused_computation.59.clone.1.clone | loop fusion | flops 18079744 | bytes 172032 | tf_op jit(solution)/shard_map/while/body/eval_jaxpr/reduce_sum | solution.py:50
  100.4 6.3 %fusion.258 = (f32[16,128]{1,0:T(8,128)S(1)}, f32[16,128]{1,0:T(8,128)S(1)}, f32[16,128]{1,0:T(8,128)S(1)}, f32[16,128]{1,0:T(8,128)S(1)}, f32[16,128]{1,0:T(8,128)S(1)}, /*index=5*/f32[16,128]{1,0:T(8,128)S(1)}) fusion(f32[16,128]{1,0:T(8,128)S(1)} %get-tuple-element.1259, f32[16,128]{1,0:T(8,128)S(1)} %get-tuple-element.1260, ...), kind=kLoop, calls=%fused_computation.27.clone.1.clone | loop fusion | flops 26726400 | bytes 196608 | tf_op jit(solution)/shard_map/while/body/eval_jaxpr/reduce_sum | solution.py:50
  106.8 4.3 %fusion.257 = (f32[16,128]{1,0:T(8,128)S(1)}, f32[16,128]{1,0:T(8,128)S(1)}, f32[16,128]{1,0:T(8,128)S(1)}, f32[16,128]{1,0:T(8,128)S(1)}) fusion(f32[16,128]{1,0:T(8,128)S(1)} %get-tuple-element.1245, f32[16,128]{1,0:T(8,128)S(1)} %get-tuple-element.1246, f32[16,128]{1,0:T(8,128)S(1)} %get-tuple-element.1226, ...), kind=kLoop, calls=%fused_computation.48.clone.1.clone | loop fusion | flops 18079744 | bytes 172032 | tf_op jit(solution)/shard_map/while/body/eval_jaxpr/reduce_sum | solution.py:50
  111.1 4.3 %fusion.256 = (f32[16,128]{1,0:T(8,128)S(1)}, f32[16,128]{1,0:T(8,128)S(1)}, f32[16,128]{1,0:T(8,128)S(1)}, f32[16,128]{1,0:T(8,128)S(1)}) fusion(f32[16,128]{1,0:T(8,128)S(1)} %get-tuple-element.1222, f32[16,128]{1,0:T(8,128)S(1)} %get-tuple-element.1223, f32[16,128]{1,0:T(8,128)S(1)} %get-tuple-element.1226, ...), kind=kLoop, calls=%fused_computation.55.clone.1.clone | loop fusion | flops 18079744 | bytes 172032 | tf_op jit(solution)/shard_map/while/body/eval_jaxpr/reduce_sum | solution.py:50
  120.7 4.3 %multiply_reduce_fusion.39 = (f32[16,128]{1,0:T(8,128)S(1)}, f32[16,128]{1,0:T(8,128)S(1)}, f32[16,128]{1,0:T(8,128)S(1)}, f32[16,128]{1,0:T(8,128)S(1)}) fusion(f32[16,128]{1,0:T(8,128)S(1)} %get-tuple-element.1276, f32[16,128]{1,0:T(8,128)S(1)} %get-tuple-element.1226, f32[16,128]{1,0:T(8,128)S(1)} %get-tuple-element.1277, ...), kind=kLoop, calls=%fused_computation.59.clone.1.clone | loop fusion | flops 18079744 | bytes 172032 | tf_op jit(solution)/shard_map/while/body/eval_jaxpr/reduce_sum | solution.py:50
  125.0 6.3 %fusion.258 = (f32[16,128]{1,0:T(8,128)S(1)}, f32[16,128]{1,0:T(8,128)S(1)}, f32[16,128]{1,0:T(8,128)S(1)}, f32[16,128]{1,0:T(8,128)S(1)}, f32[16,128]{1,0:T(8,128)S(1)}, /*index=5*/f32[16,128]{1,0:T(8,128)S(1)}) fusion(f32[16,128]{1,0:T(8,128)S(1)} %get-tuple-element.1259, f32[16,128]{1,0:T(8,128)S(1)} %get-tuple-element.1260, ...), kind=kLoop, calls=%fused_computation.27.clone.1.clone | loop fusion | flops 26726400 | bytes 196608 | tf_op jit(solution)/shard_map/while/body/eval_jaxpr/reduce_sum | solution.py:50
  131.4 4.3 %fusion.257 = (f32[16,128]{1,0:T(8,128)S(1)}, f32[16,128]{1,0:T(8,128)S(1)}, f32[16,128]{1,0:T(8,128)S(1)}, f32[16,128]{1,0:T(8,128)S(1)}) fusion(f32[16,128]{1,0:T(8,128)S(1)} %get-tuple-element.1245, f32[16,128]{1,0:T(8,128)S(1)} %get-tuple-element.1246, f32[16,128]{1,0:T(8,128)S(1)} %get-tuple-element.1226, ...), kind=kLoop, calls=%fused_computation.48.clone.1.clone | loop fusion | flops 18079744 | bytes 172032 | tf_op jit(solution)/shard_map/while/body/eval_jaxpr/reduce_sum | solution.py:50
  135.7 4.3 %fusion.256 = (f32[16,128]{1,0:T(8,128)S(1)}, f32[16,128]{1,0:T(8,128)S(1)}, f32[16,128]{1,0:T(8,128)S(1)}, f32[16,128]{1,0:T(8,128)S(1)}) fusion(f32[16,128]{1,0:T(8,128)S(1)} %get-tuple-element.1222, f32[16,128]{1,0:T(8,128)S(1)} %get-tuple-element.1223, f32[16,128]{1,0:T(8,128)S(1)} %get-tuple-element.1226, ...), kind=kLoop, calls=%fused_computation.55.clone.1.clone | loop fusion | flops 18079744 | bytes 172032 | tf_op jit(solution)/shard_map/while/body/eval_jaxpr/reduce_sum | solution.py:50
  140.7 4.1 %collective-permute-start.2 = (f32[1,16,2,128]{3,1,0,2:T(8,128)S(1)}, f32[1,16,2,128]{3,1,0,2:T(8,128)S(1)}, u32[]{:S(2)}, u32[]{:S(2)}) collective-permute-start(f32[1,16,2,128]{3,1,0,2:T(8,128)S(1)} %get-tuple-element.742), channel_id=1, source_target_pairs={{0,1},{1,2},{2,3},{3,4},{4,5},{5,6},{6,7},{7,8},{8,9},{9,10},{10,1... | collective-permute-start | bytes 49160 | tf_op jit(solution)/shard_map/ppermute | solution.py:22
  149.9 75.6 %while.35 = (s32[]{:T(128)}, f32[2,16,2,128]{3,2,1,0:T(2,128)S(1)}, s32[2]{0:T(128)S(1)}, f32[4,18,8,128]{3,1,2,0:T(8,128)S(1)}, f32[4,18,2,128]{3,1,2,0:T(8,128)S(1)}, /*index=5*/f32[]{:T(128)}) while((s32[]{:T(128)}, f32[2,16,2,128]{3,2,1,0:T(2,128)S(1)}, s32[2]{0:T(128)S(1)}, f32[4,18,8,128]{3,1,2,0:T(8,128)S(1)}, ...), condition=%wide.region_41.42_spmd.clone, body=%wide.region_22.41_spmd.sunk.clone | while | flops 107024400 | bytes 4563259 | solution.py:156
  155.6 3.7 %multiply_reduce_fusion.45 = (f32[16,128]{1,0:T(8,128)S(1)}, f32[16,128]{1,0:T(8,128)S(1)}) fusion(f32[16,128]{1,0:T(8,128)S(1)} %get-tuple-element.1424, f32[16,128]{1,0:T(8,128)S(1)} %get-tuple-element.1325, f32[16,128]{1,0:T(8,128)S(1)} %get-tuple-element.1425, f32[16,128]{1,0:T(8,128)S(1)} %get-tuple-element.1329, ...), kind=kLoop, calls=%fused_computation.401.clone.1.clone | loop fusion | flops 11792384 | bytes 155652 | tf_op jit(solution)/shard_map/while/body/eval_jaxpr/reduce_sum | solution.py:67
  159.4 3.8 %multiply_reduce_fusion.44 = (f32[16,128]{1,0:T(8,128)S(1)}, f32[16,128]{1,0:T(8,128)S(1)}) fusion(f32[16,128]{1,0:T(8,128)S(1)} %get-tuple-element.1413, f32[16,128]{1,0:T(8,128)S(1)} %get-tuple-element.1325, f32[16,128]{1,0:T(8,128)S(1)} %get-tuple-element.1414, f32[16,128]{1,0:T(8,128)S(1)} %get-tuple-element.1329, ...), kind=kLoop, calls=%fused_computation.404.clone.1.clone | loop fusion | flops 12054528 | bytes 155652 | tf_op jit(solution)/shard_map/while/body/eval_jaxpr/reduce_sum | solution.py:67
  167.0 5.4 %multiply_reduce_fusion.43 = (f32[16,128]{1,0:T(8,128)S(1)}, f32[16,128]{1,0:T(8,128)S(1)}, f32[16,128]{1,0:T(8,128)S(1)}, f32[16,128]{1,0:T(8,128)S(1)}) fusion(f32[16,128]{1,0:T(8,128)S(1)} %get-tuple-element.1384, f32[16,128]{1,0:T(8,128)S(1)} %get-tuple-element.1325, f32[16,128]{1,0:T(8,128)S(1)} %get-tuple-element.1387, ...), kind=kLoop, calls=%fused_computation.398.clone.1.clone | loop fusion | flops 23584768 | bytes 180228 | tf_op jit(solution)/shard_map/while/body/eval_jaxpr/reduce_sum | solution.py:67
  176.2 3.8 %multiply_reduce_fusion.42 = (f32[16,128]{1,0:T(8,128)S(1)}, f32[16,128]{1,0:T(8,128)S(1)}) fusion(f32[16,128]{1,0:T(8,128)S(1)} %get-tuple-element.1358, f32[16,128]{1,0:T(8,128)S(1)} %get-tuple-element.1325, f32[16,128]{1,0:T(8,128)S(1)} %get-tuple-element.1361, f32[16,128]{1,0:T(8,128)S(1)} %get-tuple-element.1329, ...), kind=kLoop, calls=%fused_computation.412.clone.1.clone | loop fusion | flops 12054528 | bytes 155652 | tf_op jit(solution)/shard_map/while/body/eval_jaxpr/reduce_sum | solution.py:67
  180.0 3.7 %multiply_reduce_fusion.41 = (f32[16,128]{1,0:T(8,128)S(1)}, f32[16,128]{1,0:T(8,128)S(1)}) fusion(f32[16,128]{1,0:T(8,128)S(1)} %get-tuple-element.1347, f32[16,128]{1,0:T(8,128)S(1)} %get-tuple-element.1325, f32[16,128]{1,0:T(8,128)S(1)} %get-tuple-element.1348, f32[16,128]{1,0:T(8,128)S(1)} %get-tuple-element.1329, ...), kind=kLoop, calls=%fused_computation.415.clone.1.clone | loop fusion | flops 11792384 | bytes 155652 | tf_op jit(solution)/shard_map/while/body/eval_jaxpr/reduce_sum | solution.py:67
  183.8 3.8 %multiply_reduce_fusion.40 = (f32[16,128]{1,0:T(8,128)S(1)}, f32[16,128]{1,0:T(8,128)S(1)}) fusion(f32[16,128]{1,0:T(8,128)S(1)} %get-tuple-element.1322, f32[16,128]{1,0:T(8,128)S(1)} %get-tuple-element.1325, f32[16,128]{1,0:T(8,128)S(1)} %get-tuple-element.1328, f32[16,128]{1,0:T(8,128)S(1)} %get-tuple-element.1329, ...), kind=kLoop, calls=%fused_computation.418.clone.1.clone | loop fusion | flops 12054528 | bytes 155652 | tf_op jit(solution)/shard_map/while/body/eval_jaxpr/reduce_sum | solution.py:67
  193.4 3.7 %multiply_reduce_fusion.45 = (f32[16,128]{1,0:T(8,128)S(1)}, f32[16,128]{1,0:T(8,128)S(1)}) fusion(f32[16,128]{1,0:T(8,128)S(1)} %get-tuple-element.1424, f32[16,128]{1,0:T(8,128)S(1)} %get-tuple-element.1325, f32[16,128]{1,0:T(8,128)S(1)} %get-tuple-element.1425, f32[16,128]{1,0:T(8,128)S(1)} %get-tuple-element.1329, ...), kind=kLoop, calls=%fused_computation.401.clone.1.clone | loop fusion | flops 11792384 | bytes 155652 | tf_op jit(solution)/shard_map/while/body/eval_jaxpr/reduce_sum | solution.py:67
  197.2 3.8 %multiply_reduce_fusion.44 = (f32[16,128]{1,0:T(8,128)S(1)}, f32[16,128]{1,0:T(8,128)S(1)}) fusion(f32[16,128]{1,0:T(8,128)S(1)} %get-tuple-element.1413, f32[16,128]{1,0:T(8,128)S(1)} %get-tuple-element.1325, f32[16,128]{1,0:T(8,128)S(1)} %get-tuple-element.1414, f32[16,128]{1,0:T(8,128)S(1)} %get-tuple-element.1329, ...), kind=kLoop, calls=%fused_computation.404.clone.1.clone | loop fusion | flops 12054528 | bytes 155652 | tf_op jit(solution)/shard_map/while/body/eval_jaxpr/reduce_sum | solution.py:67
  204.8 5.4 %multiply_reduce_fusion.43 = (f32[16,128]{1,0:T(8,128)S(1)}, f32[16,128]{1,0:T(8,128)S(1)}, f32[16,128]{1,0:T(8,128)S(1)}, f32[16,128]{1,0:T(8,128)S(1)}) fusion(f32[16,128]{1,0:T(8,128)S(1)} %get-tuple-element.1384, f32[16,128]{1,0:T(8,128)S(1)} %get-tuple-element.1325, f32[16,128]{1,0:T(8,128)S(1)} %get-tuple-element.1387, ...), kind=kLoop, calls=%fused_computation.398.clone.1.clone | loop fusion | flops 23584768 | bytes 180228 | tf_op jit(solution)/shard_map/while/body/eval_jaxpr/reduce_sum | solution.py:67
  214.0 3.8 %multiply_reduce_fusion.42 = (f32[16,128]{1,0:T(8,128)S(1)}, f32[16,128]{1,0:T(8,128)S(1)}) fusion(f32[16,128]{1,0:T(8,128)S(1)} %get-tuple-element.1358, f32[16,128]{1,0:T(8,128)S(1)} %get-tuple-element.1325, f32[16,128]{1,0:T(8,128)S(1)} %get-tuple-element.1361, f32[16,128]{1,0:T(8,128)S(1)} %get-tuple-element.1329, ...), kind=kLoop, calls=%fused_computation.412.clone.1.clone | loop fusion | flops 12054528 | bytes 155652 | tf_op jit(solution)/shard_map/while/body/eval_jaxpr/reduce_sum | solution.py:67
  221.6 3.8 %multiply_reduce_fusion.40 = (f32[16,128]{1,0:T(8,128)S(1)}, f32[16,128]{1,0:T(8,128)S(1)}) fusion(f32[16,128]{1,0:T(8,128)S(1)} %get-tuple-element.1322, f32[16,128]{1,0:T(8,128)S(1)} %get-tuple-element.1325, f32[16,128]{1,0:T(8,128)S(1)} %get-tuple-element.1328, f32[16,128]{1,0:T(8,128)S(1)} %get-tuple-element.1329, ...), kind=kLoop, calls=%fused_computation.418.clone.1.clone | loop fusion | flops 12054528 | bytes 155652 | tf_op jit(solution)/shard_map/while/body/eval_jaxpr/reduce_sum | solution.py:67
  (114 shorter events, 32.2 us)
Async XLA Ops:
  0.6 0.7 copy-start
  2.4 88.3 %collective-permute-start = (f32[1,16,8,128]{3,1,0,2:T(8,128)S(1)}, f32[1,16,8,128]{3,1,0,2:T(8,128)S(1)}, u32[]{:S(2)}, u32[]{:S(2)}) collective-permute-start(f32[1,16,8,128]{3,1,0,2:T(8,128)S(1)} %get-tuple-element.740), channel_id=1, source_target_pairs={{0,1},{1,2},{2,3},{3,4},{4,5},{5,6},{6,7},{7,8},{8,9},{9,10},{10,1... | collective-permute-start | bytes 196616 | tf_op jit(solution)/shard_map/ppermute | solution.py:22
  7.3 83.4 %collective-permute-start.1 = (f32[1,16,8,128]{3,1,0,2:T(8,128)S(1)}, f32[1,16,8,128]{3,1,0,2:T(8,128)S(1)}, u32[]{:S(2)}, u32[]{:S(2)}) collective-permute-start(f32[1,16,8,128]{3,1,0,2:T(8,128)S(1)} %get-tuple-element.741), channel_id=1, source_target_pairs={{1,0},{2,1},{3,2},{4,3},{5,4},{6,5},{7,6},{8,7},{9,8},{10,9},{11,1... | collective-permute-start | bytes 196616 | tf_op jit(solution)/shard_map/ppermute | solution.py:23
  140.7 6.6 %collective-permute-start.2 = (f32[1,16,2,128]{3,1,0,2:T(8,128)S(1)}, f32[1,16,2,128]{3,1,0,2:T(8,128)S(1)}, u32[]{:S(2)}, u32[]{:S(2)}) collective-permute-start(f32[1,16,2,128]{3,1,0,2:T(8,128)S(1)} %get-tuple-element.742), channel_id=1, source_target_pairs={{0,1},{1,2},{2,3},{3,4},{4,5},{5,6},{6,7},{7,8},{8,9},{9,10},{10,1... | collective-permute-start | bytes 49160 | tf_op jit(solution)/shard_map/ppermute | solution.py:22
  144.8 5.1 %collective-permute-start.3 = (f32[1,16,2,128]{3,1,0,2:T(8,128)S(1)}, f32[1,16,2,128]{3,1,0,2:T(8,128)S(1)}, u32[]{:S(2)}, u32[]{:S(2)}) collective-permute-start(f32[1,16,2,128]{3,1,0,2:T(8,128)S(1)} %get-tuple-element.743), channel_id=1, source_target_pairs={{1,0},{2,1},{3,2},{4,3},{5,4},{6,5},{7,6},{8,7},{9,8},{10,9},{11,1... | collective-permute-start | bytes 49160 | tf_op jit(solution)/shard_map/ppermute | solution.py:23
where the time goes:
time: 227 us; the launch traced here: 226 us
  other arithmetic  105 us (46%)
  blocking collectives  79.6 us (35%)
  loops' own time  19.6 us (9%)
  starting transfers between devices  12.8 us (6%)
  local copies, waits for them, and re-layouts  3.82 us (2%)
  waiting for transfers between devices  2.56 us (1%)
  between operations  2.47 us (1%)
    pmax x1, blocking collectives, on_device(): sound = sound_factor * lax.pmax(local_top, ('group', 'dev'))  79.6 us
    reduce_sum x16, other arithmetic, force_terms(): accel_x = -jnp.sum(weight * sep_x, axis=-1)  63.4 us
    reduce_sum x8, other arithmetic, density_terms(): jnp.sum(mass_j * closing * gradient, axis=-1)  38.5 us
    another operation x1, loops' own time, force_fields(): lax.map(force_one_block, jnp.arange(col_total * per_column, dtype=jnp.int...  10.3 us
    another operation x1, loops' own time, column_fields(): lax.map(column_one_block, jnp.arange(col_total * per_column, dtype=jnp.in...  9.28 us
    ppermute x2, starting transfers between devices, extended(): before = lax.ppermute(last, axis, up)  9 us
  transfers between devices with their start and end apart: 4, of which 1 were waited for; matrix products, arithmetic and copies ran while one was open for 0% of the time, Pallas kernels for 0%

commit v1 on v0

v1 whole, which is shorter than its diff:
```python
import functools
import math

import jax
import jax.numpy as jnp
from jax import lax
from jax.experimental import pallas as pl
from jax.experimental.pallas import tpu as pltpu
from jax.sharding import PartitionSpec as P

MESH = pl.DeviceIdType.MESH

kernel_scale = 28.0 / math.pi
gradient_scale = 140.0 / math.pi
sound_factor = 10.0
softening = 0.01 / 4.0
tiny = 1e-30

own_pairs = ((0, 0, 0), (1, 0, 1))
side_pairs = ((2, 1, -1), (3, 1, 0), (4, 1, 1))


def spread_row(row):
    return jnp.broadcast_to(row, (8, row.shape[1]))


def spread_col(col, lanes):
    return jnp.broadcast_to(col, (col.shape[0], lanes))


def column_of(row):
    n = row.shape[1]
    eye = lax.broadcasted_iota(jnp.int32, (n, n), 0) == lax.broadcasted_iota(jnp.int32, (n, n), 1)
    return jnp.sum(jnp.where(eye, jnp.broadcast_to(row, (n, n)), 0.0), axis=1, keepdims=True)


def body(
    sizes,
    p_ref,
    n_ref,
    den_ref,
    rate_ref,
    acc_ref,
    rows_t,
    cols_t,
    aux_rows,
    aux_cols,
    live_t,
    grad_t,
    visc_t,
    acc_i1,
    acc_j1,
    acc_i2,
    acc_j2,
    total_t,
    ghost,
    ghost_n,
    part1_out,
    part1_in,
    rho_out,
    rho_in,
    part2_out,
    part2_in,
    top1,
    top2,
    top_out,
    top2_out,
    send_sem,
    recv_sem,
    top1_send,
    top1_recv,
    top2_send,
    top2_recv,
):
    n_group, n_dev, block, unroll = sizes
    total = n_group * n_dev
    blocks = total // block
    n_cols, n_rows, _, slots = p_ref.shape
    me = lax.axis_index("group") * n_dev + lax.axis_index("dev")

    def coords(flat):
        return (flat // n_dev, flat % n_dev)

    right = coords((me + 1) % total)
    left = coords((me + total - 1) % total)
    offset = me % block
    which = me // block
    near = [coords(which * block + (offset + k) % block) for k in range(1, block)]
    far = [coords(((which + k) % blocks) * block + offset) for k in range(1, blocks)]

    barrier = pltpu.get_barrier_semaphore()
    for other in [left, right] + near + far:
        pl.semaphore_signal(barrier, inc=1, device_id=other, device_id_type=MESH)

    def copy_to(src, dst, send, recv, device):
        return pltpu.make_async_remote_copy(
            src_ref=src,
            dst_ref=dst,
            send_sem=send,
            recv_sem=recv,
            device_id=device,
            device_id_type=MESH,
        )

    ghost_copy = copy_to(p_ref.at[0], ghost, send_sem.at[0], recv_sem.at[0], left)
    count_copy = copy_to(n_ref, ghost_n, send_sem.at[1], recv_sem.at[1], left)
    part1_copy = copy_to(part1_out, part1_in, send_sem.at[2], recv_sem.at[2], right)
    rho_copy = copy_to(rho_out, rho_in, send_sem.at[3], recv_sem.at[3], left)
    part2_copy = copy_to(part2_out, part2_in, send_sem.at[4], recv_sem.at[4], right)

    lane_ids = lax.broadcasted_iota(jnp.int32, (n_rows, slots), 1).astype(jnp.float32)
    mass_row = lax.broadcasted_iota(jnp.int32, (8, slots), 0) == 4

    def live_of(counts_row):
        fill = column_of(counts_row.astype(jnp.float32))
        return jnp.where(lane_ids < fill, 1.0, 0.0)

    def load_cell(c, r, tile):
        live = spread_row(live_t[c, pl.ds(r, 1), :])
        return jnp.where(mass_row & (live < 0.5), 0.0, tile)

    for c in range(n_cols):
        live_t[c] = live_of(n_ref[c : c + 1, :])
    pad = jnp.where(mass_row, 0.0, 0.5)
    for c in range(n_cols + 1):
        rows_t[c, 0] = pad
        rows_t[c, n_rows + 1] = pad
        aux_rows[c, 0] = jnp.ones((8, slots), jnp.float32)
        aux_rows[c, n_rows + 1] = jnp.ones((8, slots), jnp.float32)
    acc_i1[...] = jnp.zeros_like(acc_i1)
    acc_i2[...] = jnp.zeros_like(acc_i2)

    for c in range(n_cols):

        def own_cell(r, carry, c=c):
            tile = load_cell(c, r, p_ref[c, r])
            rows_t[c, r + 1] = tile
            cols_t[c, r] = tile.T
            return carry

        lax.fori_loop(0, n_rows, own_cell, 0)

    top = jnp.zeros((n_rows, slots), jnp.float32)
    for c in range(n_cols):
        vx, vy = (p_ref[c, :, 2, :], p_ref[c, :, 3, :])
        top = jnp.maximum(top, jnp.where(live_t[c] > 0.5, vx * vx + vy * vy, 0.0))
    top_row = spread_row(jnp.max(top, axis=0, keepdims=True))
    top_out[...] = top_row
    top1[offset] = top_row

    def first_pass(c, pairs, first):
        def one_row(r, carry):
            def one_group(step, sums):
                sums = list(sums)
                for u in range(unroll):
                    at = pl.multiple_of((step * unroll + u) * 8, 8)
                    t = cols_t[c, r, pl.ds(at, 8), :]
                    xj, yj, vxj, vyj, mj, hj, cj = [
                        spread_col(t[:, k : k + 1], slots) for k in (0, 1, 2, 3, 4, 5, 7)
                    ]
                    sum_w = sum_r = None
                    for n, (slot, dc, dr) in enumerate(pairs):
                        cell = rows_t.at[c + dc, r + 1 + dr]
                        xi, yi, vxi, vyi, mi, hi, ci = [
                            spread_row(cell[k : k + 1, :]) for k in (0, 1, 2, 3, 4, 5, 7)
                        ]
                        dx = xi - (xj - dc) if dc else xi - xj
                        dy = yi - (yj - dr) if dr else yi - yj
                        inv = 1.0 / (hi + hj)
                        inv_sq = inv * inv
                        ratio_sq = (dx * dx + dy * dy) * inv_sq
                        ratio = ratio_sq * lax.rsqrt(jnp.maximum(ratio_sq, tiny))
                        fall = jnp.maximum(1.0 - ratio, 0.0)
                        base = fall * fall * fall * inv_sq * (mi * mj)
                        grad = base * inv_sq
                        kern = base * (fall * (1.25 - fall))
                        closing = (vxi - vxj) * dx + (vyi - vyj) * dy
                        rate = closing * grad
                        visc = jnp.minimum(rate, 0.0) * ((ci + cj) * inv)
                        visc = visc * (1.0 / (ratio_sq + softening))
                        grad_t[c, r, slot, pl.ds(at, 8), :] = grad
                        visc_t[c, r, slot, pl.ds(at, 8), :] = visc
                        sums[2 * n] = sums[2 * n] + kern
                        sums[2 * n + 1] = sums[2 * n + 1] + rate
                        if slot:
                            sum_w = kern if sum_w is None else sum_w + kern
                            sum_r = rate if sum_r is None else sum_r + rate
                    if first:
                        acc_j1[c, r, 0, pl.ds(at, 8), :] = sum_w
                        acc_j1[c, r, 1, pl.ds(at, 8), :] = sum_r
                    else:
                        acc_j1[c, r, 0, pl.ds(at, 8), :] += sum_w
                        acc_j1[c, r, 1, pl.ds(at, 8), :] += sum_r
                return tuple(sums)

            zero = jnp.zeros((8, slots), jnp.float32)
            sums = lax.fori_loop(0, slots // 8 // unroll, one_group, (zero,) * (2 * len(pairs)))
            for n, (slot, dc, dr) in enumerate(pairs):
                acc_i1[c + dc, r + 1 + dr, 0] += sums[2 * n]
                acc_i1[c + dc, r + 1 + dr, 1] += sums[2 * n + 1]
            return carry

        lax.fori_loop(0, n_rows, one_row, 0)

    def second_pass(c, pairs, first):
        def one_row(r, carry):
            def one_group(step, sums):
                sums = list(sums)
                for u in range(unroll):
                    at = pl.multiple_of((step * unroll + u) * 8, 8)
                    t = cols_t[c, r, pl.ds(at, 8), :]
                    a = aux_cols[c, r, pl.ds(at, 8), :]
                    xj, yj = [spread_col(t[:, k : k + 1], slots) for k in (0, 1)]
                    rho_j, press_j = [spread_col(a[:, k : k + 1], slots) for k in (0, 1)]
                    sum_x = sum_y = None
                    for n, (slot, dc, dr) in enumerate(pairs):
                        cell = rows_t.at[c + dc, r + 1 + dr]
                        aux = aux_rows.at[c + dc, r + 1 + dr]
                        xi, yi = [spread_row(cell[k : k + 1, :]) for k in (0, 1)]
                        rho_i, press_i = [spread_row(aux[k : k + 1, :]) for k in (0, 1)]
                        dx = xi - (xj - dc) if dc else xi - xj
                        dy = yi - (yj - dr) if dr else yi - yj
                        grad = grad_t[c, r, slot, pl.ds(at, 8), :]
                        visc = visc_t[c, r, slot, pl.ds(at, 8), :]
                        force = (press_i + press_j) * grad + visc * (1.0 / (rho_i + rho_j))
                        fx, fy = (force * dx, force * dy)
                        sums[2 * n] = sums[2 * n] + fx
                        sums[2 * n + 1] = sums[2 * n + 1] + fy
                        if slot:
                            sum_x = fx if sum_x is None else sum_x + fx
                            sum_y = fy if sum_y is None else sum_y + fy
                    if first:
                        acc_j2[c, r, 0, pl.ds(at, 8), :] = sum_x
                        acc_j2[c, r, 1, pl.ds(at, 8), :] = sum_y
                    else:
                        acc_j2[c, r, 0, pl.ds(at, 8), :] += sum_x
                        acc_j2[c, r, 1, pl.ds(at, 8), :] += sum_y
                return tuple(sums)

            zero = jnp.zeros((8, slots), jnp.float32)
            sums = lax.fori_loop(0, slots // 8 // unroll, one_group, (zero,) * (2 * len(pairs)))
            for n, (slot, dc, dr) in enumerate(pairs):
                acc_i2[c + dc, r + 1 + dr, 0] += sums[2 * n]
                acc_i2[c + dc, r + 1 + dr, 1] += sums[2 * n + 1]
            return carry

        lax.fori_loop(0, n_rows, one_row, 0)

    def cell_totals(c, acc_i, acc_j, sign):
        def one_row(r, carry):
            for k in range(2):
                other = acc_j[c, r, k].T.reshape(slots // 8, 8, slots).sum(axis=0)
                both = acc_i[c, r + 1, k] + sign * other
                total_t[k, pl.ds(r, 1), :] = jnp.sum(both, axis=0, keepdims=True)
            return carry

        lax.fori_loop(0, n_rows, one_row, 0)

    def ghost_totals(acc_i, out):
        def one_row(r, carry):
            for k in range(2):
                out[k, pl.ds(r, 1), :] = jnp.sum(acc_i[n_cols, r + 1, k], axis=0, keepdims=True)
            return carry

        lax.fori_loop(0, n_rows, one_row, 0)

    def store_aux(c, rho, press, own):
        total_t[0] = rho
        total_t[1] = press

        def one_row(r, carry):
            aux_rows[c, r + 1, 0:1, :] = total_t[0, pl.ds(r, 1), :]
            aux_rows[c, r + 1, 1:2, :] = total_t[1, pl.ds(r, 1), :]
            if own:
                aux_cols[c, r] = aux_rows[c, r + 1].T
            return carry

        lax.fori_loop(0, n_rows, one_row, 0)

    def finish_density(c, extra):
        cell_totals(c, acc_i1, acc_j1, 1.0)
        live = live_t[c] > 0.5
        over_mass = 1.0 / p_ref[c, :, 4, :]
        w, rate = (total_t[0], total_t[1])
        if extra is not None:
            w, rate = (w + extra[0], rate + extra[1])
        rho = w * over_mass * kernel_scale
        den_ref[c] = jnp.where(live, rho, 0.0)
        rate_ref[c] = jnp.where(live, rate * over_mass * (-gradient_scale), 0.0)
        return jnp.where(live, rho, 1.0)

    def pressure(rho, rest, live, sound):
        return jnp.where(live > 0.5, (-2.0 * sound) * (rho - rest) / (rho * rho), 0.0)

    def finish_force(c, extra, sound):
        cell_totals(c, acc_i2, acc_j2, -1.0)
        live = live_t[c] > 0.5
        scale = (-0.5 * gradient_scale * sound) / p_ref[c, :, 4, :]
        for k in range(2):
            value = total_t[k]
            if extra is not None:
                value = value + extra[k]
            acc_ref[c, :, k, :] = jnp.where(live, value * scale, 0.0)

    last = n_cols - 1

    pl.semaphore_wait(barrier, 2 + len(near) + len(far))
    ghost_copy.start()
    count_copy.start()
    near_copies = [
        copy_to(top_out, top1.at[offset], top1_send.at[k], top1_recv.at[offset], other)
        for k, other in enumerate(near)
    ]
    for copy in near_copies:
        copy.start()

    for c in range(n_cols):
        if c < last:
            first_pass(c, own_pairs, True)

    for k in range(1, block):
        sender = (offset + k) % block
        copy_to(top_out, top1.at[sender], top1_send.at[k - 1], top1_recv.at[sender], left).wait_recv()
    block_top = top1[0]
    for k in range(1, block):
        block_top = jnp.maximum(block_top, top1[k])
    top2_out[...] = block_top
    top2[which] = block_top
    far_copies = [
        copy_to(top2_out, top2.at[which], top2_send.at[k], top2_recv.at[which], other)
        for k, other in enumerate(far)
    ]
    for copy in far_copies:
        copy.start()

    ghost_copy.wait_recv()
    count_copy.wait_recv()
    inside = jnp.where(me < total - 1, 1.0, 0.0)
    live_t[n_cols] = live_of(ghost_n[0:1, :]) * inside

    def ghost_cell(r, carry):
        rows_t[n_cols, r + 1] = load_cell(n_cols, r, ghost[r])
        return carry

    lax.fori_loop(0, n_rows, ghost_cell, 0)

    first_pass(last, side_pairs, True)
    ghost_totals(acc_i1, part1_out)
    part1_copy.start()
    for c in range(last):
        first_pass(c, side_pairs, False)

    for k in range(1, blocks):
        sender = (which + k) % blocks
        copy_to(top2_out, top2.at[sender], top2_send.at[k - 1], top2_recv.at[sender], left).wait_recv()
    all_top = top2[0]
    for k in range(1, blocks):
        all_top = jnp.maximum(all_top, top2[k])
    all_top = jnp.max(all_top, axis=1, keepdims=True)
    sound_col = sound_factor * jnp.sqrt(all_top)
    sound = jnp.broadcast_to(sound_col[0:1, :], (n_rows, slots))

    part1_copy.wait_recv()
    for c in range(last):
        rho = finish_density(c, part1_in if c == 0 else None)
        if c == 0:
            rho_out[...] = rho
            rho_copy.start()
        store_aux(c, rho, pressure(rho, p_ref[c, :, 6, :], live_t[c], sound), True)
    first_pass(last, own_pairs, False)
    rho = finish_density(last, None)
    store_aux(last, rho, pressure(rho, p_ref[last, :, 6, :], live_t[last], sound), True)

    for c in range(last):
        second_pass(c, own_pairs, True)
    rho_copy.wait_recv()
    rho = rho_in[...]
    store_aux(n_cols, rho, pressure(rho, ghost[:, 6, :], live_t[n_cols], sound), False)
    second_pass(last, side_pairs, True)
    ghost_totals(acc_i2, part2_out)
    part2_copy.start()
    for c in range(last):
        second_pass(c, side_pairs, False)
    second_pass(last, own_pairs, False)
    finish_force(last, None, sound)
    part2_copy.wait_recv()
    for c in range(last):
        finish_force(c, part2_in if c == 0 else None, sound)

    for copy in [ghost_copy, count_copy, part1_copy, rho_copy, part2_copy] + near_copies + far_copies:
        copy.wait_send()


def on_device(sizes, particles, counts):
    n_group, n_dev, block, _ = sizes
    blocks = n_group * n_dev // block
    n_cols, n_rows, comps, slots = particles.shape
    f32 = jnp.float32
    vmem = pl.BlockSpec(memory_space=pltpu.VMEM)
    pair_store = pltpu.VMEM((n_cols, n_rows, 5, slots, slots), f32)
    acc_i = pltpu.VMEM((n_cols + 1, n_rows + 2, 2, 8, slots), f32)
    acc_j = pltpu.VMEM((n_cols, n_rows, 2, slots, slots), f32)
    pair_rows = pltpu.VMEM((2, n_rows, slots), f32)
    return pl.pallas_call(
        functools.partial(body, sizes),
        out_shape=(
            jax.ShapeDtypeStruct((n_cols, n_rows, slots), f32),
            jax.ShapeDtypeStruct((n_cols, n_rows, slots), f32),
            jax.ShapeDtypeStruct((n_cols, n_rows, 2, slots), f32),
        ),
        in_specs=[vmem, vmem],
        out_specs=(vmem, vmem, vmem),
        scratch_shapes=[
            pltpu.VMEM((n_cols + 1, n_rows + 2, 8, slots), f32),
            pltpu.VMEM((n_cols, n_rows, slots, 8), f32),
            pltpu.VMEM((n_cols + 1, n_rows + 2, 8, slots), f32),
            pltpu.VMEM((n_cols, n_rows, slots, 8), f32),
            pltpu.VMEM((n_cols + 1, n_rows, slots), f32),
            pair_store,
            pair_store,
            acc_i,
            acc_j,
            acc_i,
            acc_j,
            pair_rows,
            pltpu.VMEM((n_rows, 8, slots), f32),
            pltpu.VMEM(counts.shape, jnp.int32),
            pair_rows,
            pair_rows,
            pltpu.VMEM((n_rows, slots), f32),
            pltpu.VMEM((n_rows, slots), f32),
            pair_rows,
            pair_rows,
            pltpu.VMEM((block, 8, slots), f32),
            pltpu.VMEM((blocks, 8, slots), f32),
            pltpu.VMEM((8, slots), f32),
            pltpu.VMEM((8, slots), f32),
            pltpu.SemaphoreType.DMA((5,)),
            pltpu.SemaphoreType.DMA((5,)),
            pltpu.SemaphoreType.DMA((block,)),
            pltpu.SemaphoreType.DMA((block,)),
            pltpu.SemaphoreType.DMA((blocks,)),
            pltpu.SemaphoreType.DMA((blocks,)),
        ],
        compiler_params=pltpu.CompilerParams(
            collective_id=0, has_side_effects=True, vmem_limit_bytes=60 * 1024 * 1024
        ),
        name="sph",
    )(particles, counts)


def solution(mesh):
    n_group, n_dev = (mesh.shape["group"], mesh.shape["dev"])
    block = 1
    while block * block * 4 <= n_group * n_dev:
        block *= 2
    return jax.shard_map(
        functools.partial(on_device, (n_group, n_dev, block, 4)),
        mesh=mesh,
        in_specs=(P(("group", "dev"), None, None, None), P(("group", "dev"), None)),
        out_specs=(
            P(("group", "dev"), None, None),
            P(("group", "dev"), None, None),
            P(("group", "dev"), None, None, None),
        ),
        check_vma=False,
    )
```

time: 227 us -> 83.4 us (0.37)
  other arithmetic: 105 us -> 0 us
  Pallas kernels: 0 us -> 80 us
  blocking collectives: 79.6 us -> 0 us
  loops' own time: 19.6 us -> 0 us
  starting transfers between devices: 12.8 us -> 0 us
  waiting for transfers between devices: 2.56 us -> 0 us
    reduce_sum x24 -> x0, other arithmetic: 102 us -> none  [the longest x16 63.4 us: force_terms(): accel_x = -jnp.sum(weight * sep_x, axis=-1)]
    pallas_call x0 -> x1, Pallas kernels: none -> 80 us  [on_device(): pl.pallas_call(functools.partial(body, sizes), out_shape=(jax.ShapeDtypeS...]
    pmax x1 -> x0, blocking collectives: 79.6 us -> none  [on_device(): sound = sound_factor * lax.pmax(local_top, ('group', 'dev'))]
    another operation x2 -> x0, loops' own time: 19.6 us -> none  [the longest x1 10.3 us: force_fields(): lax.map(force_one_block, jnp.arange(col_total * per_column, dtype=jnp.int...]
    ppermute x4 -> x0, starting transfers between devices: 12.8 us -> none  [the longest x2 9 us: extended(): before = lax.ppermute(last, axis, up)]
    dynamic_slice x10 -> x0, local copies, waits for them, and re-layouts: 2.76 us -> none  [the longest x4 2.51 us: column_fields(): lax.map(column_one_block, jnp.arange(col_total * per_column, dtype=jnp.in...]
    ppermute x4 -> x0, waiting for transfers between devices: 2.56 us -> none  [the longest x2 2.55 us: extended(): after = lax.ppermute(first, axis, down)]
  transfers between devices with their start and end apart: 4 -> 0, of which waited for: 1 -> 0; matrix products, arithmetic and copies ran while one was open for 0% -> 0% of each run, Pallas kernels for 0% -> 0%
where the time goes in v1:
time: 83.4 us; the launch traced here: 83.2 us
  Pallas kernels  80 us (96%)
  local copies, waits for them, and re-layouts  2.56 us (3%)
    pallas_call x1, Pallas kernels, on_device(): pl.pallas_call(functools.partial(body, sizes), out_shape=(jax.ShapeDtypeS...  80 us
    unnamed x7, local copies, waits for them, and re-layouts  2.56 us

profile of v1, /device:TPU:1, one launch (start us, length us, event | category | flops | bytes accessed | tf_op | source)
XLA Modules:
  0.0 83.2 jit_solution(11492534145015774323)
XLA Ops:
  0.6 80.0 %sph.1 = (f32[2,16,128]{2,1,0:T(8,128)}, f32[2,16,128]{2,1,0:T(8,128)}, f32[2,16,2,128]{3,2,1,0:T(2,128)}) custom-call(f32[2,16,8,128]{3,2,1,0:T(8,128)} %p_ref.1, s32[2,16]{1,0:T(2,128)} %n_ref.1), custom_call_target="tpu_custom_call" | custom-call | tf_op jit(solution)/shard_map/sph/pallas_call | solution.py:404
  80.6 0.0 copy-start.1
  80.7 0.0 copy-start
  80.7 1.3 %copy.8 = f32[2,16,128]{2,1,0:T(8,128)} copy(f32[2,16,128]{2,1,0:T(8,128)} %get-tuple-element.6) | data formatting | bytes 32768
  82.0 0.0 copy-done.1
  82.0 0.6 copy.9
  82.6 0.0 copy-done
  82.6 0.6 copy.10
Async XLA Ops:
  80.6 1.4 %copy-start.1 = (f32[2,16,128]{2,1,0:T(8,128)S(1)}, f32[2,16,128]{2,1,0:T(8,128)}, u32[]{:S(2)}) copy-start(f32[2,16,128]{2,1,0:T(8,128)} %get-tuple-element.7) | copy-start | bytes 49156
  80.7 2.0 %copy-start = (f32[2,16,2,128]{3,2,1,0:T(2,128)S(1)}, f32[2,16,2,128]{3,2,1,0:T(2,128)}, u32[]{:S(2)}) copy-start(f32[2,16,2,128]{3,2,1,0:T(2,128)} %get-tuple-element.8) | copy-start | bytes 98308

commit v2 on v1

--- a/solution.py
+++ b/solution.py
@@ -24,14 +24,17 @@
     return jnp.broadcast_to(row, (8, row.shape[1]))
 
 
-def spread_col(col, lanes):
-    return jnp.broadcast_to(col, (col.shape[0], lanes))
-
-
 def column_of(row):
     n = row.shape[1]
     eye = lax.broadcasted_iota(jnp.int32, (n, n), 0) == lax.broadcasted_iota(jnp.int32, (n, n), 1)
     return jnp.sum(jnp.where(eye, jnp.broadcast_to(row, (n, n)), 0.0), axis=1, keepdims=True)
+
+
+def split(value):
+    high = value.astype(jnp.bfloat16).astype(jnp.float32)
+    rest = value - high
+    middle = rest.astype(jnp.bfloat16).astype(jnp.float32)
+    return (high, middle, rest - middle)
 
 
 def body(
@@ -41,10 +44,15 @@
     den_ref,
     rate_ref,
     acc_ref,
-    rows_t,
-    cols_t,
-    aux_rows,
-    aux_cols,
+    mean_t,
+    lhs1,
+    lhs2,
+    moved,
+    fixed,
+    steps,
+    sums_t,
+    geo1,
+    geo2,
     live_t,
     grad_t,
     visc_t,
@@ -72,7 +80,7 @@
     top2_send,
     top2_recv,
 ):
-    n_group, n_dev, block, unroll = sizes
+    n_group, n_dev, block = sizes
     total = n_group * n_dev
     blocks = total // block
     n_cols, n_rows, _, slots = p_ref.shape
@@ -115,18 +123,121 @@
         fill = column_of(counts_row.astype(jnp.float32))
         return jnp.where(lane_ids < fill, 1.0, 0.0)
 
+    row_ids = lax.broadcasted_iota(jnp.int32, (8, slots), 0)
+    zeros = jnp.zeros((8, slots), jnp.float32)
+    zeros16 = jnp.zeros((16, slots), jnp.bfloat16)
+
+    def pick(k, value, other):
+        return jnp.where(row_ids == k, value, other)
+
+    def pair_up(a, b):
+        return jnp.concatenate([a, b], axis=0).astype(jnp.bfloat16)
+
     def load_cell(c, r, tile):
         live = spread_row(live_t[c, pl.ds(r, 1), :])
-        return jnp.where(mass_row & (live < 0.5), 0.0, tile)
+        tile = jnp.where(mass_row & (live < 0.5), 0.0, tile)
+        return tile - mean_t[...]
+
+    def square_sums(tile):
+        square = tile * tile
+        turned = pltpu.roll(tile, 6, axis=0)
+        work = tile * turned
+        return (
+            spread_row(square[0:1, :] + square[1:2, :]),
+            spread_row(work[0:1, :] + work[1:2, :]),
+            turned,
+        )
+
+    def lane_side(c, row, tile, kinds):
+        at_six = [spread_row(tile[k : k + 1, :]) for k in (5, 7)]
+        plain = (
+            pick(5, 1.0, pick(6, at_six[0], 0.0)),
+            pick(7, 1.0, pick(6, at_six[1], 0.0)),
+            pick(4, tile, 0.0),
+        )
+        for q, value in enumerate(plain):
+            for level, part in enumerate(split(value)):
+                fixed[c, row, q, level] = pair_up(part, zeros)
+        for slot, dc, dr in kinds:
+            here = tile + pick(0, float(dc), pick(1, float(dr), 0.0))
+            size, work, turned = square_sums(here)
+            back = pltpu.roll(here, 2, axis=0)
+            for_size = jnp.where(row_ids < 2, -2.0 * here, pick(6, size, 0.0))
+            for_work = jnp.where(
+                row_ids < 2, -turned, jnp.where(row_ids < 4, -back, pick(6, work, 0.0))
+            )
+            for q, value in enumerate((for_size, for_work)):
+                for level, part in enumerate(split(value)):
+                    extra = pick(q, 1.0, 0.0) if level == 0 else zeros
+                    moved[c, row, slot, q, level] = pair_up(part, extra)
+            for q in range(2):
+                parts = split(spread_row(here[q : q + 1, :]))
+                parts = [pick(q, -1.0, pick(4, part, 0.0)) for part in parts]
+                steps[c, row, slot, q, 0:16] = pair_up(parts[0], parts[1])
+                steps[c, row, slot, q, 16:32] = pair_up(parts[2], zeros)
+
+    def sublane_side(c, r, tile):
+        size, work, _ = square_sums(tile)
+        first = split(pick(6, 1.0, tile))
+        second = split(pick(0, size, pick(1, work, 0.0)))
+        levels = [jnp.concatenate([a, b], axis=0) for a, b in zip(first, second)]
+        stack = [levels[k] for k in (0, 0, 0, 1, 1, 2)]
+        stack = stack + [jnp.zeros((slots - 96, slots), jnp.float32)]
+        lhs1[c, r] = jnp.concatenate(stack, axis=0).T.astype(jnp.bfloat16)
+
+    def first_rhs(c, row, slot):
+        parts = []
+        for q in range(5):
+            if q < 2:
+                levels = [moved[c, row, slot, q, k] for k in range(3)]
+            else:
+                levels = [fixed[c, row, q - 2, k] for k in range(3)]
+            stack = [levels[k] for k in (0, 1, 2, 0, 1, 0)] + [zeros16] * ((slots - 96) // 16)
+            parts.append(jnp.concatenate(stack, axis=0))
+        return jnp.concatenate(parts, axis=1)
+
+    def second_rhs(c, row, slot):
+        fill = [zeros16] * ((slots - 32) // 16)
+        parts = [jnp.concatenate([steps[c, row, slot, q]] + fill, axis=0) for q in range(2)]
+        parts += [jnp.concatenate([sums_t[c, row, q]] + fill, axis=0) for q in range(2)]
+        return jnp.concatenate(parts, axis=1)
 
     for c in range(n_cols):
         live_t[c] = live_of(n_ref[c : c + 1, :])
-    pad = jnp.where(mass_row, 0.0, 0.5)
+    top = jnp.zeros((n_rows, slots), jnp.float32)
+    count = jnp.zeros((n_rows, slots), jnp.float32)
+    mean_x = jnp.zeros((n_rows, slots), jnp.float32)
+    mean_y = jnp.zeros((n_rows, slots), jnp.float32)
+    for c in range(n_cols):
+        vx, vy = (p_ref[c, :, 2, :], p_ref[c, :, 3, :])
+        live = live_t[c]
+        top = jnp.maximum(top, jnp.where(live > 0.5, vx * vx + vy * vy, 0.0))
+        count = count + live
+        mean_x = mean_x + live * vx
+        mean_y = mean_y + live * vy
+    top_row = spread_row(jnp.max(top, axis=0, keepdims=True))
+
+    def whole_sum(value):
+        lanes = jnp.sum(value, axis=0, keepdims=True)
+        return jnp.broadcast_to(jnp.sum(spread_row(lanes), axis=1, keepdims=True), (8, slots))
+
+    share = 1.0 / jnp.maximum(whole_sum(count), 1.0)
+    mean_t[...] = jnp.where(
+        row_ids < 2,
+        0.5,
+        pick(2, whole_sum(mean_x) * share, pick(3, whole_sum(mean_y) * share, 0.0)),
+    )
+    pad = pick(5, 0.5, 0.0)
+    kinds_of = {}
     for c in range(n_cols + 1):
-        rows_t[c, 0] = pad
-        rows_t[c, n_rows + 1] = pad
-        aux_rows[c, 0] = jnp.ones((8, slots), jnp.float32)
-        aux_rows[c, n_rows + 1] = jnp.ones((8, slots), jnp.float32)
+        kinds = own_pairs if c == 0 else side_pairs if c == n_cols else own_pairs + side_pairs
+        kinds_of[c] = kinds
+        for row in (0, n_rows + 1):
+            lane_side(c, row, pad, kinds)
+            for q in range(2):
+                parts = [pick(2 + q, 1.0, pick(4, 1.0 if k == 0 and q == 0 else 0.0, 0.0)) for k in range(3)]
+                sums_t[c, row, q, 0:16] = pair_up(parts[0], parts[1])
+                sums_t[c, row, q, 16:32] = pair_up(parts[2], zeros)
     acc_i1[...] = jnp.zeros_like(acc_i1)
     acc_i2[...] = jnp.zeros_like(acc_i2)
 
@@ -134,117 +245,95 @@
 
         def own_cell(r, carry, c=c):
             tile = load_cell(c, r, p_ref[c, r])
-            rows_t[c, r + 1] = tile
-            cols_t[c, r] = tile.T
+            lane_side(c, r + 1, tile, kinds_of[c])
+            sublane_side(c, r, tile)
             return carry
 
         lax.fori_loop(0, n_rows, own_cell, 0)
 
-    top = jnp.zeros((n_rows, slots), jnp.float32)
-    for c in range(n_cols):
-        vx, vy = (p_ref[c, :, 2, :], p_ref[c, :, 3, :])
-        top = jnp.maximum(top, jnp.where(live_t[c] > 0.5, vx * vx + vy * vy, 0.0))
-    top_row = spread_row(jnp.max(top, axis=0, keepdims=True))
     top_out[...] = top_row
     top1[offset] = top_row
 
+    def run_pairs(c, pairs, lhs, rhs, geo, use):
+        depth = len(pairs)
+
+        def fill(r, n):
+            slot, dc, dr = pairs[n]
+            width = geo.shape[1]
+            out = jnp.dot(
+                lhs[c, r], rhs(c + dc, r + 1 + dr, slot), preferred_element_type=jnp.float32
+            )
+            for q in range(width):
+                geo[n, q] = out[:, q * slots : (q + 1) * slots]
+
+        def one_row(r, carry):
+            for n in range(depth):
+                if n + 1 < depth:
+                    fill(r, n + 1)
+                else:
+                    fill(jnp.minimum(r + 1, n_rows - 1), 0)
+                use(r, n)
+            return carry
+
+        fill(0, 0)
+        lax.fori_loop(0, n_rows, one_row, 0)
+
     def first_pass(c, pairs, first):
-        def one_row(r, carry):
-            def one_group(step, sums):
-                sums = list(sums)
-                for u in range(unroll):
-                    at = pl.multiple_of((step * unroll + u) * 8, 8)
-                    t = cols_t[c, r, pl.ds(at, 8), :]
-                    xj, yj, vxj, vyj, mj, hj, cj = [
-                        spread_col(t[:, k : k + 1], slots) for k in (0, 1, 2, 3, 4, 5, 7)
-                    ]
-                    sum_w = sum_r = None
-                    for n, (slot, dc, dr) in enumerate(pairs):
-                        cell = rows_t.at[c + dc, r + 1 + dr]
-                        xi, yi, vxi, vyi, mi, hi, ci = [
-                            spread_row(cell[k : k + 1, :]) for k in (0, 1, 2, 3, 4, 5, 7)
-                        ]
-                        dx = xi - (xj - dc) if dc else xi - xj
-                        dy = yi - (yj - dr) if dr else yi - yj
-                        inv = 1.0 / (hi + hj)
-                        inv_sq = inv * inv
-                        ratio_sq = (dx * dx + dy * dy) * inv_sq
-                        ratio = ratio_sq * lax.rsqrt(jnp.maximum(ratio_sq, tiny))
-                        fall = jnp.maximum(1.0 - ratio, 0.0)
-                        base = fall * fall * fall * inv_sq * (mi * mj)
-                        grad = base * inv_sq
-                        kern = base * (fall * (1.25 - fall))
-                        closing = (vxi - vxj) * dx + (vyi - vyj) * dy
-                        rate = closing * grad
-                        visc = jnp.minimum(rate, 0.0) * ((ci + cj) * inv)
-                        visc = visc * (1.0 / (ratio_sq + softening))
-                        grad_t[c, r, slot, pl.ds(at, 8), :] = grad
-                        visc_t[c, r, slot, pl.ds(at, 8), :] = visc
-                        sums[2 * n] = sums[2 * n] + kern
-                        sums[2 * n + 1] = sums[2 * n + 1] + rate
-                        if slot:
-                            sum_w = kern if sum_w is None else sum_w + kern
-                            sum_r = rate if sum_r is None else sum_r + rate
-                    if first:
-                        acc_j1[c, r, 0, pl.ds(at, 8), :] = sum_w
-                        acc_j1[c, r, 1, pl.ds(at, 8), :] = sum_r
+        def use(r, n):
+            slot, dc, dr = pairs[n]
+            total_w = total_r = zeros
+            for g in range(slots // 8):
+                at = slice(g * 8, g * 8 + 8)
+                size, closing, reach, coeff, mass = [geo1[n, q, at, :] for q in range(5)]
+                inv = 1.0 / reach
+                inv_sq = inv * inv
+                ratio_sq = jnp.maximum(size * inv_sq, tiny)
+                ratio = ratio_sq * lax.rsqrt(ratio_sq)
+                fall = jnp.maximum(1.0 - ratio, 0.0)
+                base = fall * fall * fall * (inv_sq * mass)
+                grad = base * inv_sq
+                kern = base * (fall * (1.25 - fall))
+                rate = closing * grad
+                visc = jnp.minimum(rate, 0.0) * (coeff * inv)
+                visc = visc * (1.0 / (ratio_sq + softening))
+                grad_t[c, r, slot, at, :] = grad
+                visc_t[c, r, slot, at, :] = visc
+                total_w = total_w + kern
+                total_r = total_r + rate
+                if slot:
+                    if first and n == (1 if slot == 1 else 0):
+                        acc_j1[c, r, 0, at, :] = kern
+                        acc_j1[c, r, 1, at, :] = rate
                     else:
-                        acc_j1[c, r, 0, pl.ds(at, 8), :] += sum_w
-                        acc_j1[c, r, 1, pl.ds(at, 8), :] += sum_r
-                return tuple(sums)
-
-            zero = jnp.zeros((8, slots), jnp.float32)
-            sums = lax.fori_loop(0, slots // 8 // unroll, one_group, (zero,) * (2 * len(pairs)))
-            for n, (slot, dc, dr) in enumerate(pairs):
-                acc_i1[c + dc, r + 1 + dr, 0] += sums[2 * n]
-                acc_i1[c + dc, r + 1 + dr, 1] += sums[2 * n + 1]
-            return carry
-
-        lax.fori_loop(0, n_rows, one_row, 0)
+                        acc_j1[c, r, 0, at, :] += kern
+                        acc_j1[c, r, 1, at, :] += rate
+            acc_i1[c + dc, r + 1 + dr, 0] += total_w
+            acc_i1[c + dc, r + 1 + dr, 1] += total_r
+
+        run_pairs(c, pairs, lhs1, first_rhs, geo1, use)
 
     def second_pass(c, pairs, first):
-        def one_row(r, carry):
-            def one_group(step, sums):
-                sums = list(sums)
-                for u in range(unroll):
-                    at = pl.multiple_of((step * unroll + u) * 8, 8)
-                    t = cols_t[c, r, pl.ds(at, 8), :]
-                    a = aux_cols[c, r, pl.ds(at, 8), :]
-                    xj, yj = [spread_col(t[:, k : k + 1], slots) for k in (0, 1)]
-                    rho_j, press_j = [spread_col(a[:, k : k + 1], slots) for k in (0, 1)]
-                    sum_x = sum_y = None
-                    for n, (slot, dc, dr) in enumerate(pairs):
-                        cell = rows_t.at[c + dc, r + 1 + dr]
-                        aux = aux_rows.at[c + dc, r + 1 + dr]
-                        xi, yi = [spread_row(cell[k : k + 1, :]) for k in (0, 1)]
-                        rho_i, press_i = [spread_row(aux[k : k + 1, :]) for k in (0, 1)]
-                        dx = xi - (xj - dc) if dc else xi - xj
-                        dy = yi - (yj - dr) if dr else yi - yj
-                        grad = grad_t[c, r, slot, pl.ds(at, 8), :]
-                        visc = visc_t[c, r, slot, pl.ds(at, 8), :]
-                        force = (press_i + press_j) * grad + visc * (1.0 / (rho_i + rho_j))
-                        fx, fy = (force * dx, force * dy)
-                        sums[2 * n] = sums[2 * n] + fx
-                        sums[2 * n + 1] = sums[2 * n + 1] + fy
-                        if slot:
-                            sum_x = fx if sum_x is None else sum_x + fx
-                            sum_y = fy if sum_y is None else sum_y + fy
-                    if first:
-                        acc_j2[c, r, 0, pl.ds(at, 8), :] = sum_x
-                        acc_j2[c, r, 1, pl.ds(at, 8), :] = sum_y
+        def use(r, n):
+            slot, dc, dr = pairs[n]
+            total_x = total_y = zeros
+            for g in range(slots // 8):
+                at = slice(g * 8, g * 8 + 8)
+                dx, dy, rho, press = [geo2[n, q, at, :] for q in range(4)]
+                force = press * grad_t[c, r, slot, at, :] + visc_t[c, r, slot, at, :] * (1.0 / rho)
+                fx, fy = (force * dx, force * dy)
+                total_x = total_x + fx
+                total_y = total_y + fy
+                if slot:
+                    if first and n == (1 if slot == 1 else 0):
+                        acc_j2[c, r, 0, at, :] = fx
+                        acc_j2[c, r, 1, at, :] = fy
                     else:
-                        acc_j2[c, r, 0, pl.ds(at, 8), :] += sum_x
-                        acc_j2[c, r, 1, pl.ds(at, 8), :] += sum_y
-                return tuple(sums)
-
-            zero = jnp.zeros((8, slots), jnp.float32)
-            sums = lax.fori_loop(0, slots // 8 // unroll, one_group, (zero,) * (2 * len(pairs)))
-            for n, (slot, dc, dr) in enumerate(pairs):
-                acc_i2[c + dc, r + 1 + dr, 0] += sums[2 * n]
-                acc_i2[c + dc, r + 1 + dr, 1] += sums[2 * n + 1]
-            return carry
-
-        lax.fori_loop(0, n_rows, one_row, 0)
+                        acc_j2[c, r, 0, at, :] += fx
+                        acc_j2[c, r, 1, at, :] += fy
+            acc_i2[c + dc, r + 1 + dr, 0] += total_x
+            acc_i2[c + dc, r + 1 + dr, 1] += total_y
+
+        run_pairs(c, pairs, lhs2, second_rhs, geo2, use)
 
     def cell_totals(c, acc_i, acc_j, sign):
         def one_row(r, carry):
@@ -269,10 +358,19 @@
         total_t[1] = press
 
         def one_row(r, carry):
-            aux_rows[c, r + 1, 0:1, :] = total_t[0, pl.ds(r, 1), :]
-            aux_rows[c, r + 1, 1:2, :] = total_t[1, pl.ds(r, 1), :]
+            both = [total_t[k, pl.ds(r, 1), :] for k in range(2)]
+            for q in range(2):
+                parts = split(spread_row(both[q]))
+                parts = [pick(2 + q, 1.0, pick(4, part, 0.0)) for part in parts]
+                sums_t[c, r + 1, q, 0:16] = pair_up(parts[0], parts[1])
+                sums_t[c, r + 1, q, 16:32] = pair_up(parts[2], zeros)
             if own:
-                aux_cols[c, r] = aux_rows[c, r + 1].T
+                tile = p_ref[c, r] - mean_t[...]
+                tile = jnp.where(row_ids < 2, tile, 0.0)
+                tile = pick(2, spread_row(both[0]), pick(3, spread_row(both[1]), tile))
+                parts = [pick(4, 1.0, part) for part in split(tile)]
+                stack = parts + [jnp.zeros((slots - 24, slots), jnp.float32)]
+                lhs2[c, r] = jnp.concatenate(stack, axis=0).T.astype(jnp.bfloat16)
             return carry
 
         lax.fori_loop(0, n_rows, one_row, 0)
@@ -339,7 +437,7 @@
     live_t[n_cols] = live_of(ghost_n[0:1, :]) * inside
 
     def ghost_cell(r, carry):
-        rows_t[n_cols, r + 1] = load_cell(n_cols, r, ghost[r])
+        lane_side(n_cols, r + 1, load_cell(n_cols, r, ghost[r]), kinds_of[n_cols])
         return carry
 
     lax.fori_loop(0, n_rows, ghost_cell, 0)
@@ -392,10 +490,10 @@
 
 
 def on_device(sizes, particles, counts):
-    n_group, n_dev, block, _ = sizes
+    n_group, n_dev, block = sizes
     blocks = n_group * n_dev // block
     n_cols, n_rows, comps, slots = particles.shape
-    f32 = jnp.float32
+    f32, bf16 = (jnp.float32, jnp.bfloat16)
     vmem = pl.BlockSpec(memory_space=pltpu.VMEM)
     pair_store = pltpu.VMEM((n_cols, n_rows, 5, slots, slots), f32)
     acc_i = pltpu.VMEM((n_cols + 1, n_rows + 2, 2, 8, slots), f32)
@@ -411,10 +509,15 @@
         in_specs=[vmem, vmem],
         out_specs=(vmem, vmem, vmem),
         scratch_shapes=[
-            pltpu.VMEM((n_cols + 1, n_rows + 2, 8, slots), f32),
-            pltpu.VMEM((n_cols, n_rows, slots, 8), f32),
-            pltpu.VMEM((n_cols + 1, n_rows + 2, 8, slots), f32),
-            pltpu.VMEM((n_cols, n_rows, slots, 8), f32),
+            pltpu.VMEM((8, slots), f32),
+            pltpu.VMEM((n_cols, n_rows, slots, slots), bf16),
+            pltpu.VMEM((n_cols, n_rows, slots, slots), bf16),
+            pltpu.VMEM((n_cols + 1, n_rows + 2, 5, 2, 3, 16, slots), bf16),
+            pltpu.VMEM((n_cols + 1, n_rows + 2, 3, 3, 16, slots), bf16),
+            pltpu.VMEM((n_cols + 1, n_rows + 2, 5, 2, 32, slots), bf16),
+            pltpu.VMEM((n_cols + 1, n_rows + 2, 2, 32, slots), bf16),
+            pltpu.VMEM((3, 5, slots, slots), f32),
+            pltpu.VMEM((3, 4, slots, slots), f32),
             pltpu.VMEM((n_cols + 1, n_rows, slots), f32),
             pair_store,
             pair_store,
@@ -455,7 +558,7 @@
     while block * block * 4 <= n_group * n_dev:
         block *= 2
     return jax.shard_map(
-        functools.partial(on_device, (n_group, n_dev, block, 4)),
+        functools.partial(on_device, (n_group, n_dev, block)),
         mesh=mesh,
         in_specs=(P(("group", "dev"), None, None, None), P(("group", "dev"), None)),
         out_specs=(

time: 83.4 us -> 64.5 us (0.77)
  Pallas kernels: 80 us -> 61.1 us
    pallas_call x1, Pallas kernels: 80 us -> 61.1 us  [on_device(): pl.pallas_call(functools.partial(body, sizes), out_shape=(jax.ShapeDtypeS...]
where the time goes in v2:
time: 64.5 us; the launch traced here: 64.4 us
  Pallas kernels  61.1 us (95%)
  local copies, waits for them, and re-layouts  2.56 us (4%)
  between operations  0.66 us (1%)
    pallas_call x1, Pallas kernels, on_device(): pl.pallas_call(functools.partial(body, sizes), out_shape=(jax.ShapeDtypeS...  61.1 us
    unnamed x7, local copies, waits for them, and re-layouts  2.56 us

profile of v2, /device:TPU:1, one launch (start us, length us, event | category | flops | bytes accessed | tf_op | source)
XLA Modules:
  0.0 64.4 jit_solution(14967648038367502008)
XLA Ops:
  0.6 61.1 %sph.1 = (f32[2,16,128]{2,1,0:T(8,128)}, f32[2,16,128]{2,1,0:T(8,128)}, f32[2,16,2,128]{3,2,1,0:T(2,128)}) custom-call(f32[2,16,8,128]{3,2,1,0:T(8,128)} %p_ref.1, s32[2,16]{1,0:T(2,128)} %n_ref.1), custom_call_target="tpu_custom_call" | custom-call | tf_op jit(solution)/shard_map/sph/pallas_call | solution.py:502
  61.8 0.0 copy-start.1
  61.8 0.0 copy-start
  61.8 1.3 %copy.8 = f32[2,16,128]{2,1,0:T(8,128)} copy(f32[2,16,128]{2,1,0:T(8,128)} %get-tuple-element.6) | data formatting | bytes 32768
  63.1 0.0 copy-done.1
  63.1 0.6 copy.9
  63.7 0.0 copy-done
  63.7 0.6 copy.10
Async XLA Ops:
  61.8 1.4 %copy-start.1 = (f32[2,16,128]{2,1,0:T(8,128)S(1)}, f32[2,16,128]{2,1,0:T(8,128)}, u32[]{:S(2)}) copy-start(f32[2,16,128]{2,1,0:T(8,128)} %get-tuple-element.7) | copy-start | bytes 49156
  61.8 2.0 %copy-start = (f32[2,16,2,128]{3,2,1,0:T(2,128)S(1)}, f32[2,16,2,128]{3,2,1,0:T(2,128)}, u32[]{:S(2)}) copy-start(f32[2,16,2,128]{3,2,1,0:T(2,128)} %get-tuple-element.8) | copy-start | bytes 98308

commit v3 on v2

v3 whole, which is shorter than its diff:
```python
import functools
import math

import jax
import jax.numpy as jnp
from jax import lax
from jax.experimental import pallas as pl
from jax.experimental.pallas import tpu as pltpu
from jax.sharding import PartitionSpec as P

MESH = pl.DeviceIdType.MESH

kernel_scale = 28.0 / math.pi
gradient_scale = 140.0 / math.pi
sound_factor = 10.0
softening = 0.01 / 4.0
tiny = 1e-30

own_pairs = ((0, 0, 0), (1, 0, 1))
side_pairs = ((2, 1, -1), (3, 1, 0), (4, 1, 1))


def spread_row(row):
    return jnp.broadcast_to(row, (8, row.shape[1]))


def column_of(row):
    n = row.shape[1]
    eye = lax.broadcasted_iota(jnp.int32, (n, n), 0) == lax.broadcasted_iota(jnp.int32, (n, n), 1)
    return jnp.sum(jnp.where(eye, jnp.broadcast_to(row, (n, n)), 0.0), axis=1, keepdims=True)


def split(value):
    high = value.astype(jnp.bfloat16).astype(jnp.float32)
    rest = value - high
    middle = rest.astype(jnp.bfloat16).astype(jnp.float32)
    return (high, middle, rest - middle)


def body(
    sizes,
    p_ref,
    n_ref,
    den_ref,
    rate_ref,
    acc_ref,
    mean_t,
    lhs1,
    moved,
    fixed,
    rows_t,
    cols_t,
    aux_rows,
    aux_cols,
    live_t,
    grad_t,
    visc_t,
    acc_i1,
    acc_j1,
    acc_i2,
    acc_j2,
    total_t,
    ghost,
    ghost_n,
    part1_out,
    part1_in,
    rho_out,
    rho_in,
    part2_out,
    part2_in,
    top1,
    top2,
    top_out,
    top2_out,
    send_sem,
    recv_sem,
    top1_send,
    top1_recv,
    top2_send,
    top2_recv,
):
    n_group, n_dev, block = sizes
    total = n_group * n_dev
    blocks = total // block
    n_cols, n_rows, _, slots = p_ref.shape
    me = lax.axis_index("group") * n_dev + lax.axis_index("dev")

    def coords(flat):
        return (lax.div(flat, n_dev), lax.rem(flat, n_dev))

    right = coords(lax.rem(me + 1, total))
    left = coords(lax.rem(me + total - 1, total))
    offset = lax.rem(me, block)
    which = lax.div(me, block)
    near = [coords(which * block + lax.rem(offset + k, block)) for k in range(1, block)]
    far = [coords(lax.rem(which + k, blocks) * block + offset) for k in range(1, blocks)]

    barrier = pltpu.get_barrier_semaphore()
    for other in [left, right] + near + far:
        pl.semaphore_signal(barrier, inc=1, device_id=other, device_id_type=MESH)

    def copy_to(src, dst, send, recv, device):
        return pltpu.make_async_remote_copy(
            src_ref=src,
            dst_ref=dst,
            send_sem=send,
            recv_sem=recv,
            device_id=device,
            device_id_type=MESH,
        )

    ghost_copy = copy_to(p_ref.at[0], ghost, send_sem.at[0], recv_sem.at[0], left)
    count_copy = copy_to(n_ref, ghost_n, send_sem.at[1], recv_sem.at[1], left)
    part1_copy = copy_to(part1_out, part1_in, send_sem.at[2], recv_sem.at[2], right)
    rho_copy = copy_to(rho_out, rho_in, send_sem.at[3], recv_sem.at[3], left)
    part2_copy = copy_to(part2_out, part2_in, send_sem.at[4], recv_sem.at[4], right)

    lane_ids = lax.broadcasted_iota(jnp.int32, (n_rows, slots), 1).astype(jnp.float32)
    mass_row = lax.broadcasted_iota(jnp.int32, (8, slots), 0) == 4

    def live_of(counts_row):
        fill = column_of(counts_row.astype(jnp.float32))
        return jnp.where(lane_ids < fill, 1.0, 0.0)

    row_ids = lax.broadcasted_iota(jnp.int32, (8, slots), 0)
    zeros = jnp.zeros((8, slots), jnp.float32)
    zeros16 = jnp.zeros((16, slots), jnp.bfloat16)

    def pick(k, value, other):
        return jnp.where(row_ids == k, value, other)

    def pair_up(a, b):
        return jnp.concatenate([a, b], axis=0).astype(jnp.bfloat16)

    def load_cell(c, r, tile):
        live = spread_row(live_t[c, pl.ds(r, 1), :])
        tile = jnp.where(mass_row & (live < 0.5), 0.0, tile)
        return tile - mean_t[...]

    def own_terms(tile):
        weight = jnp.where(row_ids < 2, 1.0, pick(5, softening, 0.0))
        square = jnp.sum(tile * tile * weight, axis=0, keepdims=True)
        turned = pltpu.roll(tile, 6, axis=0)
        product = tile * turned
        work = product[0:1, :] + product[1:2, :]
        reach = tile[5:6, :]
        return (
            spread_row(square),
            spread_row(reach * reach),
            spread_row(work),
            spread_row(reach * tile[7:8, :]),
            turned,
        )

    def lane_side(c, row, tile, kinds):
        _, reach_sq, _, viscous, _ = own_terms(tile)
        reach, coeff = [spread_row(tile[k : k + 1, :]) for k in (5, 7)]
        plain = (
            pick(5, 2.0 * reach, pick(6, reach_sq, 0.0)),
            pick(5, coeff, pick(6, viscous, pick(7, reach, 0.0))),
        )
        rows_t[c, row] = tile
        for q, value in enumerate(plain):
            for level, part in enumerate(split(value)):
                extra = pick((1, 3)[q], 1.0, 0.0) if level == 0 else zeros
                fixed[c, row, q, level] = pair_up(part, extra)
        for slot, dc, dr in kinds:
            here = tile + pick(0, float(dc), pick(1, float(dr), 0.0))
            size, _, work, _, turned = own_terms(here)
            back = pltpu.roll(here, 2, axis=0)
            for_size = jnp.where(
                row_ids < 2,
                -2.0 * here,
                pick(5, (2.0 * softening) * here, pick(6, size, 0.0)),
            )
            for_work = jnp.where(
                row_ids < 2, -turned, jnp.where(row_ids < 4, -back, pick(6, work, 0.0))
            )
            for q, value in enumerate((for_size, for_work)):
                for level, part in enumerate(split(value)):
                    extra = pick(2 * q, 1.0, 0.0) if level == 0 else zeros
                    moved[c, row, slot, q, level] = pair_up(part, extra)

    def sublane_side(c, r, tile):
        size, reach_sq, work, viscous, _ = own_terms(tile)
        first = split(pick(6, 1.0, tile))
        second = split(
            pick(0, size, pick(1, reach_sq, pick(2, work, pick(3, viscous, 0.0))))
        )
        levels = [jnp.concatenate([a, b], axis=0) for a, b in zip(first, second)]
        stack = [levels[k] for k in (0, 0, 0, 1, 1, 2)]
        stack = stack + [jnp.zeros((slots - 96, slots), jnp.float32)]
        lhs1[c, r] = jnp.concatenate(stack, axis=0).T.astype(jnp.bfloat16)
        turned = tile.T
        for q, k in enumerate((0, 1, 4)):
            cols_t[c, r, q] = jnp.broadcast_to(turned[:, k : k + 1], (slots, slots))

    def first_rhs(c, row, slot):
        parts = []
        for q in range(4):
            if q < 2:
                levels = [moved[c, row, slot, q, k] for k in range(3)]
            else:
                levels = [fixed[c, row, q - 2, k] for k in range(3)]
            stack = [levels[k] for k in (0, 1, 2, 0, 1, 0)] + [zeros16] * ((slots - 96) // 16)
            parts.append(jnp.concatenate(stack, axis=0))
        return jnp.concatenate(parts, axis=1)

    for c in range(n_cols):
        live_t[c] = live_of(n_ref[c : c + 1, :])
    top = jnp.zeros((n_rows, slots), jnp.float32)
    count = jnp.zeros((n_rows, slots), jnp.float32)
    mean_x = jnp.zeros((n_rows, slots), jnp.float32)
    mean_y = jnp.zeros((n_rows, slots), jnp.float32)
    for c in range(n_cols):
        vx, vy = (p_ref[c, :, 2, :], p_ref[c, :, 3, :])
        live = live_t[c]
        top = jnp.maximum(top, jnp.where(live > 0.5, vx * vx + vy * vy, 0.0))
        count = count + live
        mean_x = mean_x + live * vx
        mean_y = mean_y + live * vy
    top_row = spread_row(jnp.max(top, axis=0, keepdims=True))

    def whole_sum(value):
        lanes = jnp.sum(value, axis=0, keepdims=True)
        return jnp.broadcast_to(jnp.sum(spread_row(lanes), axis=1, keepdims=True), (8, slots))

    share = 1.0 / jnp.maximum(whole_sum(count), 1.0)
    mean_t[...] = jnp.where(
        row_ids < 2,
        0.5,
        pick(2, whole_sum(mean_x) * share, pick(3, whole_sum(mean_y) * share, 0.0)),
    )
    kinds_of = {}
    for c in range(n_cols + 1):
        kinds = own_pairs if c == 0 else side_pairs if c == n_cols else own_pairs + side_pairs
        kinds_of[c] = kinds
    acc_i1[...] = jnp.zeros_like(acc_i1)
    acc_i2[...] = jnp.zeros_like(acc_i2)

    for c in range(n_cols):

        def own_cell(r, carry, c=c):
            tile = load_cell(c, r, p_ref[c, r])
            lane_side(c, r, tile, kinds_of[c])
            sublane_side(c, r, tile)
            return carry

        lax.fori_loop(0, n_rows, own_cell, 0, unroll=2)

    top_out[...] = top_row
    top1[offset] = top_row

    def run_pairs(c, own, store, use, clear):
        dc = 0 if own else 1
        last_row = n_rows - 1

        def one_row(r, carry):
            if own:
                use(c, r, 0, 0, r, None)
                use(c, r, 1, 0, r + 1, store)
            else:
                use(c, r + 1, 2, 1, r, store)
                use(c, r, 4, 1, r + 1, False)
                use(c, r + 1, 3, 1, r + 1, False)
            return carry

        if not own:
            use(c, 0, 3, 1, 0, store)
        lax.fori_loop(0, last_row, one_row, 0)
        if own:
            use(c, last_row, 0, 0, last_row, None)
            if store:
                clear[c, last_row] = jnp.zeros((2, slots, slots), jnp.float32)

    step_of = {slot: (dc, dr) for slot, dc, dr in own_pairs + side_pairs}

    def first_use(c, r, slot, dc, i_row, store):
        out = jnp.dot(
            lhs1[c, r], first_rhs(c + dc, i_row, slot), preferred_element_type=jnp.float32
        )
        mass_i = spread_row(rows_t[c + dc, i_row, 4:5, :])
        total_w = total_r = zeros
        for g in range(slots // 8):
            at = slice(g * 8, g * 8 + 8)
            size, closing, reach_sq, coeff = [out[at, q * slots : (q + 1) * slots] for q in range(4)]
            inv_sq = 1.0 / reach_sq
            ratio_sq = jnp.maximum(size * inv_sq - softening, tiny)
            ratio = ratio_sq * lax.rsqrt(ratio_sq)
            fall = jnp.maximum(1.0 - ratio, 0.0)
            base = fall * fall * fall * (inv_sq * (mass_i * cols_t[c, r, 2, at, :]))
            grad = base * inv_sq
            kern = base * (fall * (1.25 - fall))
            rate = closing * grad
            visc = jnp.minimum(rate, 0.0) * (coeff * (1.0 / size))
            grad_t[c, r, slot, at, :] = grad
            visc_t[c, r, slot, at, :] = visc
            total_w = total_w + kern
            total_r = total_r + rate
            if store:
                acc_j1[c, r, 0, at, :] = kern
                acc_j1[c, r, 1, at, :] = rate
            elif store is not None:
                acc_j1[c, r, 0, at, :] += kern
                acc_j1[c, r, 1, at, :] += rate
        acc_i1[c + dc, i_row, 0] += total_w
        acc_i1[c + dc, i_row, 1] += total_r

    def second_use(c, r, slot, dc, i_row, store):
        xi, yi = [
            spread_row(rows_t[c + dc, i_row, k : k + 1, :]) + float(step_of[slot][k])
            for k in range(2)
        ]
        rho_i, press_i = [spread_row(aux_rows[c + dc, i_row, k : k + 1, :]) for k in range(2)]
        total_x = total_y = zeros
        for g in range(slots // 8):
            at = slice(g * 8, g * 8 + 8)
            dx = xi - cols_t[c, r, 0, at, :]
            dy = yi - cols_t[c, r, 1, at, :]
            rho = rho_i + aux_cols[c, r, 0, at, :]
            press = press_i + aux_cols[c, r, 1, at, :]
            force = press * grad_t[c, r, slot, at, :] + visc_t[c, r, slot, at, :] * (1.0 / rho)
            fx, fy = (force * dx, force * dy)
            total_x = total_x + fx
            total_y = total_y + fy
            if store:
                acc_j2[c, r, 0, at, :] = fx
                acc_j2[c, r, 1, at, :] = fy
            elif store is not None:
                acc_j2[c, r, 0, at, :] += fx
                acc_j2[c, r, 1, at, :] += fy
        acc_i2[c + dc, i_row, 0] += total_x
        acc_i2[c + dc, i_row, 1] += total_y

    def first_pass(c, own, store):
        run_pairs(c, own, store, first_use, acc_j1)

    def second_pass(c, own, store):
        run_pairs(c, own, store, second_use, acc_j2)

    def cell_totals(c, acc_i, acc_j, sign):
        def one_row(r, carry):
            for k in range(2):
                other = acc_j[c, r, k].T.reshape(slots // 8, 8, slots).sum(axis=0)
                both = acc_i[c, r, k] + sign * other
                total_t[k, pl.ds(r, 1), :] = jnp.sum(both, axis=0, keepdims=True)
            return carry

        lax.fori_loop(0, n_rows, one_row, 0, unroll=4)

    def ghost_totals(acc_i, out):
        def one_row(r, carry):
            for k in range(2):
                out[k, pl.ds(r, 1), :] = jnp.sum(acc_i[n_cols, r, k], axis=0, keepdims=True)
            return carry

        lax.fori_loop(0, n_rows, one_row, 0, unroll=4)

    def store_aux(c, rho, press, own):
        total_t[0] = rho
        total_t[1] = press

        def one_row(r, carry):
            rows = [spread_row(total_t[k, pl.ds(r, 1), :]) for k in range(2)]
            tile = pick(0, rows[0], rows[1])
            aux_rows[c, r] = tile
            if own:
                turned = tile.T
                for k in range(2):
                    aux_cols[c, r, k] = jnp.broadcast_to(turned[:, k : k + 1], (slots, slots))
            return carry

        lax.fori_loop(0, n_rows, one_row, 0, unroll=4)

    def finish_density(c, extra):
        cell_totals(c, acc_i1, acc_j1, 1.0)
        live = live_t[c] > 0.5
        over_mass = 1.0 / p_ref[c, :, 4, :]
        w, rate = (total_t[0], total_t[1])
        if extra is not None:
            w, rate = (w + extra[0], rate + extra[1])
        rho = w * over_mass * kernel_scale
        den_ref[c] = jnp.where(live, rho, 0.0)
        rate_ref[c] = jnp.where(live, rate * over_mass * (-gradient_scale), 0.0)
        return jnp.where(live, rho, 1.0)

    def pressure(rho, rest, live, sound):
        return jnp.where(live > 0.5, (-2.0 * sound) * (rho - rest) / (rho * rho), 0.0)

    def finish_force(c, extra, sound):
        cell_totals(c, acc_i2, acc_j2, -1.0)
        live = live_t[c] > 0.5
        scale = (-0.5 * gradient_scale * sound) / p_ref[c, :, 4, :]
        for k in range(2):
            value = total_t[k]
            if extra is not None:
                value = value + extra[k]
            acc_ref[c, :, k, :] = jnp.where(live, value * scale, 0.0)

    last = n_cols - 1

    pl.semaphore_wait(barrier, 2 + len(near) + len(far))
    ghost_copy.start()
    count_copy.start()
    near_copies = [
        copy_to(top_out, top1.at[offset], top1_send.at[k], top1_recv.at[offset], other)
        for k, other in enumerate(near)
    ]
    for copy in near_copies:
        copy.start()

    for c in range(n_cols):
        if c < last:
            first_pass(c, True, True)

    for k in range(1, block):
        sender = lax.rem(offset + k, block)
        copy_to(top_out, top1.at[sender], top1_send.at[k - 1], top1_recv.at[sender], left).wait_recv()
    block_top = top1[0]
    for k in range(1, block):
        block_top = jnp.maximum(block_top, top1[k])
    top2_out[...] = block_top
    top2[which] = block_top
    far_copies = [
        copy_to(top2_out, top2.at[which], top2_send.at[k], top2_recv.at[which], other)
        for k, other in enumerate(far)
    ]
    for copy in far_copies:
        copy.start()

    ghost_copy.wait_recv()
    count_copy.wait_recv()
    inside = jnp.where(me < total - 1, 1.0, 0.0)
    live_t[n_cols] = live_of(ghost_n[0:1, :]) * inside

    def ghost_cell(r, carry):
        lane_side(n_cols, r, load_cell(n_cols, r, ghost[r]), kinds_of[n_cols])
        return carry

    lax.fori_loop(0, n_rows, ghost_cell, 0, unroll=2)

    first_pass(last, False, True)
    ghost_totals(acc_i1, part1_out)
    part1_copy.start()
    for c in range(last):
        first_pass(c, False, False)

    for k in range(1, blocks):
        sender = lax.rem(which + k, blocks)
        copy_to(top2_out, top2.at[sender], top2_send.at[k - 1], top2_recv.at[sender], left).wait_recv()
    all_top = top2[0]
    for k in range(1, blocks):
        all_top = jnp.maximum(all_top, top2[k])
    all_top = jnp.max(all_top, axis=1, keepdims=True)
    sound_col = sound_factor * jnp.sqrt(all_top)
    sound = jnp.broadcast_to(sound_col[0:1, :], (n_rows, slots))

    part1_copy.wait_recv()
    for c in range(last):
        rho = finish_density(c, part1_in if c == 0 else None)
        if c == 0:
            rho_out[...] = rho
            rho_copy.start()
        store_aux(c, rho, pressure(rho, p_ref[c, :, 6, :], live_t[c], sound), True)
    first_pass(last, True, False)
    rho = finish_density(last, None)
    store_aux(last, rho, pressure(rho, p_ref[last, :, 6, :], live_t[last], sound), True)

    for c in range(last):
        second_pass(c, True, True)
    rho_copy.wait_recv()
    rho = rho_in[...]
    store_aux(n_cols, rho, pressure(rho, ghost[:, 6, :], live_t[n_cols], sound), False)
    second_pass(last, False, True)
    ghost_totals(acc_i2, part2_out)
    part2_copy.start()
    for c in range(last):
        second_pass(c, False, False)
    second_pass(last, True, False)
    finish_force(last, None, sound)
    part2_copy.wait_recv()
    for c in range(last):
        finish_force(c, part2_in if c == 0 else None, sound)

    for copy in [ghost_copy, count_copy, part1_copy, rho_copy, part2_copy] + near_copies + far_copies:
        copy.wait_send()


def on_device(sizes, particles, counts):
    n_group, n_dev, block = sizes
    blocks = n_group * n_dev // block
    n_cols, n_rows, comps, slots = particles.shape
    f32, bf16 = (jnp.float32, jnp.bfloat16)
    vmem = pl.BlockSpec(memory_space=pltpu.VMEM)
    pair_store = pltpu.VMEM((n_cols, n_rows, 5, slots, slots), f32)
    acc_i = pltpu.VMEM((n_cols + 1, n_rows, 2, 8, slots), f32)
    acc_j = pltpu.VMEM((n_cols, n_rows, 2, slots, slots), f32)
    pair_rows = pltpu.VMEM((2, n_rows, slots), f32)
    return pl.pallas_call(
        functools.partial(body, sizes),
        out_shape=(
            jax.ShapeDtypeStruct((n_cols, n_rows, slots), f32),
            jax.ShapeDtypeStruct((n_cols, n_rows, slots), f32),
            jax.ShapeDtypeStruct((n_cols, n_rows, 2, slots), f32),
        ),
        in_specs=[vmem, vmem],
        out_specs=(vmem, vmem, vmem),
        scratch_shapes=[
            pltpu.VMEM((8, slots), f32),
            pltpu.VMEM((n_cols, n_rows, slots, slots), bf16),
            pltpu.VMEM((n_cols + 1, n_rows, 5, 2, 3, 16, slots), bf16),
            pltpu.VMEM((n_cols + 1, n_rows, 2, 3, 16, slots), bf16),
            pltpu.VMEM((n_cols + 1, n_rows, 8, slots), f32),
            pltpu.VMEM((n_cols, n_rows, 3, slots, slots), f32),
            pltpu.VMEM((n_cols + 1, n_rows, 8, slots), f32),
            pltpu.VMEM((n_cols, n_rows, 2, slots, slots), f32),
            pltpu.VMEM((n_cols + 1, n_rows, slots), f32),
            pair_store,
            pair_store,
            acc_i,
            acc_j,
            acc_i,
            acc_j,
            pair_rows,
            pltpu.VMEM((n_rows, 8, slots), f32),
            pltpu.VMEM(counts.shape, jnp.int32),
            pair_rows,
            pair_rows,
            pltpu.VMEM((n_rows, slots), f32),
            pltpu.VMEM((n_rows, slots), f32),
            pair_rows,
            pair_rows,
            pltpu.VMEM((block, 8, slots), f32),
            pltpu.VMEM((blocks, 8, slots), f32),
            pltpu.VMEM((8, slots), f32),
            pltpu.VMEM((8, slots), f32),
            pltpu.SemaphoreType.DMA((5,)),
            pltpu.SemaphoreType.DMA((5,)),
            pltpu.SemaphoreType.DMA((block,)),
            pltpu.SemaphoreType.DMA((block,)),
            pltpu.SemaphoreType.DMA((blocks,)),
            pltpu.SemaphoreType.DMA((blocks,)),
        ],
        compiler_params=pltpu.CompilerParams(
            collective_id=0, has_side_effects=True, vmem_limit_bytes=60 * 1024 * 1024
        ),
        name="sph",
    )(particles, counts)


def solution(mesh):
    n_group, n_dev = (mesh.shape["group"], mesh.shape["dev"])
    block = 1
    while block * block * 4 <= n_group * n_dev:
        block *= 2
    return jax.shard_map(
        functools.partial(on_device, (n_group, n_dev, block)),
        mesh=mesh,
        in_specs=(P(("group", "dev"), None, None, None), P(("group", "dev"), None)),
        out_specs=(
            P(("group", "dev"), None, None),
            P(("group", "dev"), None, None),
            P(("group", "dev"), None, None, None),
        ),
        check_vma=False,
    )
```

time: 64.5 us -> 50.4 us (0.78)
  Pallas kernels: 61.1 us -> 47 us
    pallas_call x1, Pallas kernels: 61.1 us -> 47 us  [on_device(): pl.pallas_call(functools.partial(body, sizes), out_shape=(jax.ShapeDtypeS...]
where the time goes in v3:
time: 50.4 us; the launch traced here: 50.2 us
  Pallas kernels  47 us (93%)
  local copies, waits for them, and re-layouts  2.56 us (5%)
  between operations  0.66 us (1%)
    pallas_call x1, Pallas kernels, on_device(): pl.pallas_call(functools.partial(body, sizes), out_shape=(jax.ShapeDtypeS...  47 us
    unnamed x7, local copies, waits for them, and re-layouts  2.56 us

profile of v3, /device:TPU:1, one launch (start us, length us, event | category | flops | bytes accessed | tf_op | source)
XLA Modules:
  0.0 50.2 jit_solution(11208247721567037990)
XLA Ops:
  0.6 47.0 %sph.1 = (f32[2,16,128]{2,1,0:T(8,128)}, f32[2,16,128]{2,1,0:T(8,128)}, f32[2,16,2,128]{3,2,1,0:T(2,128)}) custom-call(f32[2,16,8,128]{3,2,1,0:T(8,128)} %p_ref.1, s32[2,16]{1,0:T(2,128)} %n_ref.1), custom_call_target="tpu_custom_call" | custom-call | tf_op jit(solution)/shard_map/sph/pallas_call | solution.py:499
  47.6 0.0 copy-start.1
  47.6 0.0 copy-start
  47.6 1.3 %copy.8 = f32[2,16,128]{2,1,0:T(8,128)} copy(f32[2,16,128]{2,1,0:T(8,128)} %get-tuple-element.6) | data formatting | bytes 32768
  49.0 0.0 copy-done.1
  49.0 0.6 %copy.9 = f32[2,16,128]{2,1,0:T(8,128)} copy(f32[2,16,128]{2,1,0:T(8,128)S(1)} %copy-done.1) | data formatting | bytes 32768
  49.6 0.0 copy-done
  49.6 0.6 %copy.10 = f32[2,16,2,128]{3,2,1,0:T(2,128)} copy(f32[2,16,2,128]{3,2,1,0:T(2,128)S(1)} %copy-done) | data formatting | bytes 65536
Async XLA Ops:
  47.6 1.4 %copy-start.1 = (f32[2,16,128]{2,1,0:T(8,128)S(1)}, f32[2,16,128]{2,1,0:T(8,128)}, u32[]{:S(2)}) copy-start(f32[2,16,128]{2,1,0:T(8,128)} %get-tuple-element.7) | copy-start | bytes 49156
  47.6 2.0 %copy-start = (f32[2,16,2,128]{3,2,1,0:T(2,128)S(1)}, f32[2,16,2,128]{3,2,1,0:T(2,128)}, u32[]{:S(2)}) copy-start(f32[2,16,2,128]{3,2,1,0:T(2,128)} %get-tuple-element.8) | copy-start | bytes 98308
